TPU v7x, 32 devices: a whole 2x2x4 slice. The times are simulated.
32 devices in a mesh: seq: 16 (over z, x, core), wshard: 2 (over y).
Axes of the slice: x: 2, y: 2, z: 4, core: 2. Of those that a mesh axis runs over, the one named last changes fastest.
Arguments:
- inputs: bfloat16 [8192, 640], P(('seq', 'wshard')), may hold values from -6 to 6
- doc_ids: int32 [8192], P(('seq', 'wshard')), may hold values from 0 to 2, never falling along the last dimension, each value on 1 to 4096 neighbouring positions
- w_query: bfloat16 [640, 1024], P('wshard'), may hold values from -0.25 to 0.25
- w_key: bfloat16 [640, 256], P('wshard'), may hold values from -0.25 to 0.25
- w_value: bfloat16 [640, 256], P('wshard'), may hold values from -0.25 to 0.25
- w_out: bfloat16 [1024, 640], P('wshard'), may hold values from -0.1875 to 0.1875
- w_gate: bfloat16 [640, 2048], P('wshard'), may hold values from -0.25 to 0.25
- w_up: bfloat16 [640, 2048], P('wshard'), may hold values from -0.25 to 0.25
- w_down: bfloat16 [2048, 640], P('wshard'), may hold values from -0.125 to 0.125
- gain_in: bfloat16 [640], P('wshard'), may hold values from -0.5 to 1
- gain_attn_post: bfloat16 [640], P('wshard'), may hold values from -0.5 to 1
- gain_ff_pre: bfloat16 [640], P('wshard'), may hold values from -0.5 to 1
- gain_ff_post: bfloat16 [640], P('wshard'), may hold values from -0.5 to 1
- gain_query: bfloat16 [256], P('wshard'), may hold values from -0.5 to 1
- gain_key: bfloat16 [256], P('wshard'), may hold values from -0.5 to 1
- cotangent: bfloat16 [8192, 640], P(('seq', 'wshard')), may hold values from -6 to 6
Outputs:
- layer_out: bfloat16 [8192, 640], P(('seq', 'wshard'))
- grad_inputs: float32 [8192, 640], P(('seq', 'wshard'))
- grad_w_query: float32 [640, 1024], P('wshard')
- grad_w_key: float32 [640, 256], P('wshard')
- grad_w_value: float32 [640, 256], P('wshard')
- grad_w_out: float32 [1024, 640], P('wshard')
- grad_w_gate: float32 [640, 2048], P('wshard')
- grad_w_up: float32 [640, 2048], P('wshard')
- grad_w_down: float32 [2048, 640], P('wshard')
- grad_gain_in: float32 [640], P('wshard')
- grad_gain_attn_post: float32 [640], P('wshard')
- grad_gain_ff_pre: float32 [640], P('wshard')
- grad_gain_ff_post: float32 [640], P('wshard')
- grad_gain_query: float32 [256], P('wshard')
- grad_gain_key: float32 [256], P('wshard')
Inputs may be any that keep to these rules, and one draw needn't show every extreme that they name: `doc_ids`: document numbers never fall along the token stream; every document has 1 to 4096 tokens, one exactly 4096.
All inputs are finite; a program needn't handle non-finite values.
Results may differ from a plain program's by a relative error of at most 0.025.
Values may be sent and summed in bfloat16 or wider, within the bound.
A program may use at most 128 MiB of HBM per device.

v0:
```python
import jax
import jax.numpy as jnp
from jax import lax
from jax.sharding import PartitionSpec as P

WINDOW = 512


NORM_EPSILON = 1e-06
ROPE_BASE = 10000.0
MASK_FLOOR = -1e30


def from_behind(array, axis, by):
    count = lax.axis_size(axis)
    pairs = [(i, i + by) for i in range(count) if 0 <= i + by < count]
    return lax.ppermute(array, axis, pairs)


def rms_gain(tensor, gain_vec):
    factor = lax.rsqrt(jnp.mean(tensor * tensor, axis=-1, keepdims=True) + NORM_EPSILON)
    return tensor * factor * (1.0 + gain_vec)


def rope_tables(positions, head_width):
    half_width = head_width // 2
    exponent = jnp.arange(half_width, dtype=jnp.float32) * (2.0 / head_width)
    inverse = jnp.exp(-jnp.log(ROPE_BASE) * exponent)
    angles = positions.astype(jnp.float32)[:, None] * inverse[None, :]
    return (jnp.cos(angles), jnp.sin(angles))


def norm_rope(tensor, gain_vec, cos_table, sin_table):
    normed = rms_gain(tensor, gain_vec)
    half_width = tensor.shape[-1] // 2
    front_part = normed[..., :half_width]
    back_part = normed[..., half_width:]
    cos_rows = cos_table[:, None, :]
    sin_rows = sin_table[:, None, :]
    return jnp.concatenate(
        [
            front_part * cos_rows - back_part * sin_rows,
            back_part * cos_rows + front_part * sin_rows,
        ],
        axis=-1,
    )


def geglu(gate_pre, up_pre):
    return jax.nn.gelu(gate_pre, approximate=True) * up_pre


def window_mask(query_pos, key_pos, query_doc, key_doc):
    distance = query_pos[:, None] - key_pos[None, :]
    return (
        (distance >= 0)
        & (distance < WINDOW)
        & (key_pos[None, :] >= 0)
        & (query_doc[:, None] == key_doc[None, :])
    )


def masked_scores(queries, all_keys, allowed, score_scale):
    scores = (
        jnp.einsum("qhd,kd->hqk", queries, all_keys, preferred_element_type=jnp.float32)
        * score_scale
    )
    return jnp.where(allowed[None], scores, MASK_FLOOR)


def weight_grad(left_rows, right_rows):
    return jnp.einsum("tc,tf->cf", left_rows, right_rows, preferred_element_type=jnp.float32)


def per_device(
    inputs,
    doc_ids,
    w_query,
    w_key,
    w_value,
    w_out,
    w_gate,
    w_up,
    w_down,
    gain_in,
    gain_attn_post,
    gain_ff_pre,
    gain_ff_post,
    gain_query,
    gain_key,
    cotangent,
):
    gathered = (
        lax.all_gather(w_query, "wshard", axis=0, tiled=True),
        lax.all_gather(w_key, "wshard", axis=0, tiled=True),
        lax.all_gather(w_value, "wshard", axis=0, tiled=True),
        lax.all_gather(w_out, "wshard", axis=0, tiled=True),
        lax.all_gather(w_gate, "wshard", axis=0, tiled=True),
        lax.all_gather(w_up, "wshard", axis=0, tiled=True),
        lax.all_gather(w_down, "wshard", axis=0, tiled=True),
        lax.all_gather(gain_in, "wshard", axis=0, tiled=True),
        lax.all_gather(gain_attn_post, "wshard", axis=0, tiled=True),
        lax.all_gather(gain_ff_pre, "wshard", axis=0, tiled=True),
        lax.all_gather(gain_ff_post, "wshard", axis=0, tiled=True),
        lax.all_gather(gain_query, "wshard", axis=0, tiled=True),
        lax.all_gather(gain_key, "wshard", axis=0, tiled=True),
    )
    full_query, full_key, full_value, full_out, full_gate, full_up, full_down = gathered[:7]
    in_gain, attn_post_gain, ff_pre_gain, ff_post_gain, query_gain, key_gain = [
        g.astype(jnp.float32) for g in gathered[7:]
    ]
    row_count = inputs.shape[0]
    head_dim = full_key.shape[1]
    head_count = full_query.shape[1] // head_dim
    score_scale = head_dim ** (-0.5)
    start_row = lax.axis_index(("seq", "wshard")) * row_count
    query_pos = start_row + jnp.arange(row_count, dtype=jnp.int32)
    cos_table, sin_table = rope_tables(query_pos, head_dim)
    x_float = inputs.astype(jnp.float32)
    normed_in = rms_gain(x_float, in_gain).astype(jnp.bfloat16)
    query_raw = jnp.dot(normed_in, full_query, preferred_element_type=jnp.float32).reshape(
        row_count, head_count, head_dim
    )
    key_raw = jnp.dot(normed_in, full_key, preferred_element_type=jnp.float32)[:, None, :]
    values = jnp.dot(normed_in, full_value, preferred_element_type=jnp.float32).astype(jnp.bfloat16)
    queries = norm_rope(query_raw, query_gain, cos_table, sin_table).astype(jnp.bfloat16)
    key_rot = norm_rope(key_raw, key_gain, cos_table, sin_table)[:, 0].astype(jnp.bfloat16)
    sent_rows = min(WINDOW, row_count)
    hop_count = WINDOW // sent_rows
    outgoing = (key_rot, values, doc_ids)
    halo_keys = []
    halo_values = []
    halo_docs = []
    for distance in range(hop_count, 0, -1):
        arrived = from_behind((outgoing[0], outgoing[1], outgoing[2]), ("seq", "wshard"), distance)
        halo_keys.append(arrived[0])
        halo_values.append(arrived[1])
        halo_docs.append(arrived[2])
    all_keys = jnp.concatenate(halo_keys + [key_rot], 0)
    all_values = jnp.concatenate(halo_values + [values], 0)
    all_docs = jnp.concatenate(halo_docs + [doc_ids], 0)
    key_pos = start_row - WINDOW + jnp.arange(WINDOW + row_count, dtype=jnp.int32)
    allowed = window_mask(query_pos, key_pos, doc_ids, all_docs)
    scores = masked_scores(queries, all_keys, allowed, score_scale)
    row_peak = jnp.max(scores, axis=-1, keepdims=True)
    row_total = jnp.sum(
        jnp.where(allowed[None], jnp.exp(scores - row_peak), 0.0), axis=-1, keepdims=True
    )
    log_total = row_peak + jnp.log(row_total)
    soft = jnp.where(allowed[None], jnp.exp(scores - log_total), 0.0).astype(jnp.bfloat16)
    attended = jnp.einsum("hqk,kd->qhd", soft, all_values, preferred_element_type=jnp.float32)
    attended = attended.reshape(row_count, head_count * head_dim).astype(jnp.bfloat16)
    attn_proj = jnp.dot(attended, full_out, preferred_element_type=jnp.float32)
    resid = x_float + rms_gain(attn_proj, attn_post_gain)
    normed_ff = rms_gain(resid, ff_pre_gain).astype(jnp.bfloat16)
    gate_pre = jnp.dot(normed_ff, full_gate, preferred_element_type=jnp.float32)
    up_pre = jnp.dot(normed_ff, full_up, preferred_element_type=jnp.float32)
    hidden = geglu(gate_pre, up_pre).astype(jnp.bfloat16)
    ff_proj = jnp.dot(hidden, full_down, preferred_element_type=jnp.float32)
    layer_out = (resid + rms_gain(ff_proj, ff_post_gain)).astype(jnp.bfloat16)
    grad_top = cotangent.astype(jnp.float32)
    _, pullback = jax.vjp(rms_gain, ff_proj, ff_post_gain)
    grad_ff_proj, grad_gain_ff_post = pullback(grad_top)
    grad_ff_proj = grad_ff_proj.astype(jnp.bfloat16)
    grad_w_down = weight_grad(hidden, grad_ff_proj)
    grad_hidden = lax.dot_general(
        grad_ff_proj, full_down, (((1,), (1,)), ((), ())), preferred_element_type=jnp.float32
    )
    _, pullback = jax.vjp(geglu, gate_pre, up_pre)
    grad_gate, grad_up = pullback(grad_hidden)
    grad_gate = grad_gate.astype(jnp.bfloat16)
    grad_up = grad_up.astype(jnp.bfloat16)
    grad_w_gate = weight_grad(normed_ff, grad_gate)
    grad_w_up = weight_grad(normed_ff, grad_up)
    grad_normed_ff = lax.dot_general(
        grad_gate, full_gate, (((1,), (1,)), ((), ())), preferred_element_type=jnp.float32
    )
    grad_normed_ff = grad_normed_ff + lax.dot_general(
        grad_up, full_up, (((1,), (1,)), ((), ())), preferred_element_type=jnp.float32
    )
    _, pullback = jax.vjp(rms_gain, resid, ff_pre_gain)
    grad_resid_part, grad_gain_ff_pre = pullback(grad_normed_ff)
    grad_resid = grad_top + grad_resid_part
    ff_gradients = (grad_w_gate, grad_w_up, grad_w_down, grad_gain_ff_pre, grad_gain_ff_post)
    ff_parts = (
        lax.psum_scatter(
            ff_gradients[0].astype(jnp.bfloat16), "wshard", scatter_dimension=0, tiled=True
        ).astype(jnp.float32),
        lax.psum_scatter(
            ff_gradients[1].astype(jnp.bfloat16), "wshard", scatter_dimension=0, tiled=True
        ).astype(jnp.float32),
        lax.psum_scatter(
            ff_gradients[2].astype(jnp.bfloat16), "wshard", scatter_dimension=0, tiled=True
        ).astype(jnp.float32),
        lax.psum_scatter(
            ff_gradients[3].astype(jnp.bfloat16), "wshard", scatter_dimension=0, tiled=True
        ).astype(jnp.float32),
        lax.psum_scatter(
            ff_gradients[4].astype(jnp.bfloat16), "wshard", scatter_dimension=0, tiled=True
        ).astype(jnp.float32),
    )
    ff_reduced = (
        lax.psum(ff_parts[0].astype(jnp.bfloat16), "seq").astype(jnp.float32),
        lax.psum(ff_parts[1].astype(jnp.bfloat16), "seq").astype(jnp.float32),
        lax.psum(ff_parts[2].astype(jnp.bfloat16), "seq").astype(jnp.float32),
        lax.psum(ff_parts[3].astype(jnp.bfloat16), "seq").astype(jnp.float32),
        lax.psum(ff_parts[4].astype(jnp.bfloat16), "seq").astype(jnp.float32),
    )
    _, pullback = jax.vjp(rms_gain, attn_proj, attn_post_gain)
    grad_attn_proj, grad_gain_attn_post = pullback(grad_resid)
    grad_attn_proj = grad_attn_proj.astype(jnp.bfloat16)
    grad_w_out = weight_grad(attended, grad_attn_proj)
    grad_attended = lax.dot_general(
        grad_attn_proj, full_out, (((1,), (1,)), ((), ())), preferred_element_type=jnp.float32
    ).astype(jnp.bfloat16)
    grad_heads = grad_attended.reshape(row_count, head_count, head_dim)
    again_scores = masked_scores(queries, all_keys, allowed, score_scale)
    probs = jnp.where(allowed[None], jnp.exp(again_scores - log_total), 0.0)
    grad_soft = jnp.einsum(
        "qhd,kd->hqk", grad_heads, all_values, preferred_element_type=jnp.float32
    )
    row_inner = jnp.sum(probs * grad_soft, axis=-1, keepdims=True)
    grad_score = (probs * (grad_soft - row_inner) * score_scale).astype(jnp.bfloat16)
    grad_queries = jnp.einsum(
        "hqk,kd->qhd", grad_score, all_keys, preferred_element_type=jnp.float32
    )
    grad_keys_all = jnp.einsum(
        "hqk,qhd->kd", grad_score, queries, preferred_element_type=jnp.float32
    )
    grad_values_all = jnp.einsum(
        "hqk,qhd->kd", probs.astype(jnp.bfloat16), grad_heads, preferred_element_type=jnp.float32
    )
    back_keys = jnp.zeros((sent_rows, head_dim), jnp.float32)
    back_values = jnp.zeros((sent_rows, head_dim), jnp.float32)
    for piece_index in range(hop_count):
        distance = hop_count - piece_index
        piece_start = piece_index * sent_rows
        arrived = (
            from_behind(
                grad_keys_all[piece_start : piece_start + sent_rows].astype(jnp.bfloat16),
                ("seq", "wshard"),
                -distance,
            ).astype(jnp.float32),
            from_behind(
                grad_values_all[piece_start : piece_start + sent_rows].astype(jnp.bfloat16),
                ("seq", "wshard"),
                -distance,
            ).astype(jnp.float32),
        )
        back_keys = back_keys + arrived[0]
        back_values = back_values + arrived[1]
    own_keys = grad_keys_all[WINDOW:]
    own_values = grad_values_all[WINDOW:]
    split_row = row_count - sent_rows
    grad_keys = jnp.concatenate([own_keys[:split_row], own_keys + back_keys], 0)
    grad_values = jnp.concatenate([own_values[:split_row], own_values + back_values], 0).astype(
        jnp.bfloat16
    )

    def query_path(tensor, gain_vec):
        return norm_rope(tensor, gain_vec, cos_table, sin_table)

    _, pullback = jax.vjp(query_path, query_raw, query_gain)
    grad_query_raw, grad_gain_query = pullback(grad_queries)
    _, pullback = jax.vjp(query_path, key_raw, key_gain)
    grad_key_raw, grad_gain_key = pullback(grad_keys[:, None, :])
    grad_query_raw = grad_query_raw.reshape(row_count, head_count * head_dim).astype(jnp.bfloat16)
    grad_key_raw = grad_key_raw[:, 0].astype(jnp.bfloat16)
    grad_w_query = weight_grad(normed_in, grad_query_raw)
    grad_w_key = weight_grad(normed_in, grad_key_raw)
    grad_w_value = weight_grad(normed_in, grad_values)
    grad_normed_in = lax.dot_general(
        grad_query_raw, full_query, (((1,), (1,)), ((), ())), preferred_element_type=jnp.float32
    )
    grad_normed_in = grad_normed_in + lax.dot_general(
        grad_key_raw, full_key, (((1,), (1,)), ((), ())), preferred_element_type=jnp.float32
    )
    grad_normed_in = grad_normed_in + lax.dot_general(
        grad_values, full_value, (((1,), (1,)), ((), ())), preferred_element_type=jnp.float32
    )
    _, pullback = jax.vjp(rms_gain, x_float, in_gain)
    grad_input_part, grad_gain_in = pullback(grad_normed_in)
    grad_inputs = grad_resid + grad_input_part
    attn_gradients = (
        grad_w_query,
        grad_w_key,
        grad_w_value,
        grad_w_out,
        grad_gain_in,
        grad_gain_attn_post,
        grad_gain_query,
        grad_gain_key,
    )
    attn_parts = (
        lax.psum_scatter(
            attn_gradients[0].astype(jnp.bfloat16), "wshard", scatter_dimension=0, tiled=True
        ).astype(jnp.float32),
        lax.psum_scatter(
            attn_gradients[1].astype(jnp.bfloat16), "wshard", scatter_dimension=0, tiled=True
        ).astype(jnp.float32),
        lax.psum_scatter(
            attn_gradients[2].astype(jnp.bfloat16), "wshard", scatter_dimension=0, tiled=True
        ).astype(jnp.float32),
        lax.psum_scatter(
            attn_gradients[3].astype(jnp.bfloat16), "wshard", scatter_dimension=0, tiled=True
        ).astype(jnp.float32),
        lax.psum_scatter(
            attn_gradients[4].astype(jnp.bfloat16), "wshard", scatter_dimension=0, tiled=True
        ).astype(jnp.float32),
        lax.psum_scatter(
            attn_gradients[5].astype(jnp.bfloat16), "wshard", scatter_dimension=0, tiled=True
        ).astype(jnp.float32),
        lax.psum_scatter(
            attn_gradients[6].astype(jnp.bfloat16), "wshard", scatter_dimension=0, tiled=True
        ).astype(jnp.float32),
        lax.psum_scatter(
            attn_gradients[7].astype(jnp.bfloat16), "wshard", scatter_dimension=0, tiled=True
        ).astype(jnp.float32),
    )
    attn_reduced = (
        lax.psum(attn_parts[0].astype(jnp.bfloat16), "seq").astype(jnp.float32),
        lax.psum(attn_parts[1].astype(jnp.bfloat16), "seq").astype(jnp.float32),
        lax.psum(attn_parts[2].astype(jnp.bfloat16), "seq").astype(jnp.float32),
        lax.psum(attn_parts[3].astype(jnp.bfloat16), "seq").astype(jnp.float32),
        lax.psum(attn_parts[4].astype(jnp.bfloat16), "seq").astype(jnp.float32),
        lax.psum(attn_parts[5].astype(jnp.bfloat16), "seq").astype(jnp.float32),
        lax.psum(attn_parts[6].astype(jnp.bfloat16), "seq").astype(jnp.float32),
        lax.psum(attn_parts[7].astype(jnp.bfloat16), "seq").astype(jnp.float32),
    )
    reduced = (
        attn_reduced[0],
        attn_reduced[1],
        attn_reduced[2],
        attn_reduced[3],
        ff_reduced[0],
        ff_reduced[1],
        ff_reduced[2],
        attn_reduced[4],
        attn_reduced[5],
        ff_reduced[3],
        ff_reduced[4],
        attn_reduced[6],
        attn_reduced[7],
    )
    return (layer_out, grad_inputs) + tuple(reduced)


def solution(mesh):
    return jax.shard_map(
        per_device,
        mesh=mesh,
        in_specs=(
            P(("seq", "wshard"), None),
            P(("seq", "wshard")),
            P("wshard", None),
            P("wshard", None),
            P("wshard", None),
            P("wshard", None),
            P("wshard", None),
            P("wshard", None),
            P("wshard", None),
            P("wshard"),
            P("wshard"),
            P("wshard"),
            P("wshard"),
            P("wshard"),
            P("wshard"),
            P(("seq", "wshard"), None),
        ),
        out_specs=(
            P(("seq", "wshard"), None),
            P(("seq", "wshard"), None),
            P("wshard", None),
            P("wshard", None),
            P("wshard", None),
            P("wshard", None),
            P("wshard", None),
            P("wshard", None),
            P("wshard", None),
            P("wshard"),
            P("wshard"),
            P("wshard"),
            P("wshard"),
            P("wshard"),
            P("wshard"),
        ),
        check_vma=False,
    )
```

profile of v0, /device:TPU:0, one launch (start us, length us, event | category | flops | bytes accessed | tf_op | source)
XLA Modules:
  0.0 601.2 jit_solution(15135593721052747924)
XLA Ops:
  12.4 5.9 all-reduce.17
  18.3 9.8 %all_gather.40 = bf16[640,256]{1,0:T(8,128)(2,1)S(1)} all-gather(bf16[320,256]{1,0:T(8,128)(2,1)S(1)} %copy-done.40), channel_id=1, replica_groups=mesh['seq'=16,'wshard'=2] {'wshard'}, dimensions={0}, use_global_device_ids=true | all-gather | bytes 491520 | tf_op jit(solution)/shard_map/all_gather | solution.py:96
  29.1 4.4 collective-permute-start.1
  34.9 3.1 collective-permute-start.3
  38.0 2.8 collective-permute-start.2
  40.8 4.2 all-gather
  45.0 7.2 %all_gather.41 = bf16[640,256]{1,0:T(8,128)(2,1)S(1)} all-gather(bf16[320,256]{1,0:T(8,128)(2,1)S(1)} %copy-done.41), channel_id=1, replica_groups=mesh['seq'=16,'wshard'=2] {'wshard'}, dimensions={0}, use_global_device_ids=true | all-gather | bytes 491520 | tf_op jit(solution)/shard_map/all_gather | solution.py:95
  54.7 4.3 collective-permute-start.5
  59.7 5.4 all-gather.1
  78.5 33.6 %all-gather.12.cloned.1.call-done = bf16[640,2048]{1,0:T(8,128)(2,1)} async-done(((bf16[320,2048]{1,0:T(8,128)(2,1)}), bf16[640,2048]{1,0:T(8,128)(2,1)}) %all-gather.12.cloned.1.call-update) | async-done | bytes 2621456 | tf_op jit(solution)/shard_map/all_gather | solution.py:98
  112.1 4.0 fusion.93
  116.2 36.4 %all-gather.14.cloned.1.call-done = bf16[640,2048]{1,0:T(8,128)(2,1)} async-done(((bf16[320,2048]{1,0:T(8,128)(2,1)}), bf16[640,2048]{1,0:T(8,128)(2,1)}) %all-gather.14.cloned.1.call-update) | async-done | bytes 2621456 | tf_op jit(solution)/shard_map/all_gather | solution.py:99
  152.6 5.2 multiply_convert_fusion.1
  157.8 35.2 %all-gather.16.cloned.1.call-done = bf16[2048,640]{1,0:T(8,128)(2,1)} async-done(((bf16[1024,640]{1,0:T(8,128)(2,1)}), bf16[2048,640]{1,0:T(8,128)(2,1)}) %all-gather.16.cloned.1.call-update) | async-done | bytes 2621456 | tf_op jit(solution)/shard_map/all_gather | solution.py:100
  193.0 3.3 multiply_reduce_fusion.6
  198.0 2.5 multiply_convert_fusion
  209.1 2.3 fusion.39
  211.4 8.0 %fusion.91 = (bf16[768,256]{0,1:T(8,128)(2,1)S(1)}, f32[768,256]{0,1:T(8,128)}) fusion(bf16[256,4,128]{2,0,1:T(8,128)(2,1)} %copy-done.39, bf16[256,4,128]{2,0,1:T(8,128)(2,1)S(1)} %copy-done.38, f32[768,256,4]{1,0,2:T(8,128)} %fusion.39, f32[4,256]{1,0:T(4,128)S(1)} %log_add_fusion, f32[768,256,4]{1,0,2:T(8,128)} %copy-done.7, ...), kind=kOutput, calls=%fused_computation.183 | convolution fusion | flops 414123776 | bytes 8196096 | tf_op jit(solution)/shard_map/hqk,qhd->kd/dot_general | solution.py:227
  222.8 8.2 %fusion.15 = f32[256,4,256]{2,0,1:T(8,128)} fusion(f32[768,256,4]{1,0,2:T(8,128)} %fusion.39, bf16[256,256]{0,1:T(8,128)(2,1)} %maximum_bitcast_fusion.6, bf16[256,256]{0,1:T(8,128)(2,1)} %collective-permute-done.5, bf16[256,256]{0,1:T(8,128)(2,1)} %collective-permute-done.4, f32[768,256,4]{1,0,2:T(8,128)} %copy-done.7, f32[4,256]{1,0:T(4,128)S(1)} %log_add_fusion, ...), kind=kOutput, calls=%fused_computation.31 | convolution fusion | flops 414058240 | bytes 7933952 | tf_op jit(solution)/shard_map/hqk,kd->qhd/dot_general | solution.py:224
  251.8 2.4 convolution_convert_fusion.2
  255.4 2.4 convolution_convert_fusion.1
  259.1 2.5 convolution_convert_fusion
  261.7 11.3 %reduce-scatter.12.cloned.1.call-done = bf16[320,256]{1,0:T(8,128)(2,1)} async-done(((bf16[640,256]{1,0:T(8,128)(2,1)}), bf16[320,256]{1,0:T(8,128)(2,1)}) %reduce-scatter.12.cloned.1.call-update) | async-done | bytes 163856 | tf_op jit(solution)/shard_map/reduce_scatter | solution.py:301
  273.1 26.1 %reduce-scatter.8.cloned.1.call-done = bf16[320,1024]{1,0:T(8,128)(2,1)} async-done(((bf16[640,1024]{1,0:T(8,128)(2,1)}), bf16[320,1024]{1,0:T(8,128)(2,1)}) %reduce-scatter.8.cloned.1.call-update) | async-done | bytes 655376 | tf_op jit(solution)/shard_map/reduce_scatter | solution.py:295
  299.2 26.1 %reduce-scatter.14.cloned.1.call-done = bf16[512,640]{1,0:T(8,128)(2,1)} async-done(((bf16[1024,640]{1,0:T(8,128)(2,1)}), bf16[512,640]{1,0:T(8,128)(2,1)}) %reduce-scatter.14.cloned.1.call-update) | async-done | bytes 655376 | tf_op jit(solution)/shard_map/reduce_scatter | solution.py:304
  325.3 40.4 %reduce-scatter.16.cloned.1.call-done = bf16[320,2048]{1,0:T(8,128)(2,1)} async-done(((bf16[640,2048]{1,0:T(8,128)(2,1)}), bf16[320,2048]{1,0:T(8,128)(2,1)}) %reduce-scatter.16.cloned.1.call-update) | async-done | bytes 1310736 | tf_op jit(solution)/shard_map/reduce_scatter | solution.py:186
  365.7 40.5 %reduce-scatter.18.cloned.1.call-done = bf16[320,2048]{1,0:T(8,128)(2,1)} async-done(((bf16[640,2048]{1,0:T(8,128)(2,1)}), bf16[320,2048]{1,0:T(8,128)(2,1)}) %reduce-scatter.18.cloned.1.call-update) | async-done | bytes 1310736 | tf_op jit(solution)/shard_map/reduce_scatter | solution.py:189
  406.2 40.4 %reduce-scatter.20.cloned.1.call-done = bf16[1024,640]{1,0:T(8,128)(2,1)} async-done(((bf16[2048,640]{1,0:T(8,128)(2,1)}), bf16[1024,640]{1,0:T(8,128)(2,1)}) %reduce-scatter.20.cloned.1.call-update) | async-done | bytes 1310736 | tf_op jit(solution)/shard_map/reduce_scatter | solution.py:192
  450.4 5.1 all-reduce.16
  455.9 34.5 %all-reduce.14 = (bf16[320]{0:T(512)(128)(2,1)S(1)}, bf16[320]{0:T(512)(128)(2,1)S(1)}, bf16[320]{0:T(512)(128)(2,1)S(1)}, bf16[320]{0:T(512)(128)(2,1)S(1)}, bf...) all-reduce(bf16[320]{0:T(512)(128)(2,1)S(1)} %dynamic-slice.5, ...), channel_id=1, replica_groups=mesh['seq'=16,'wshard'=2] {'seq'}, use_global_device_ids=true, to_apply=%region_31.32 | all-reduce | flops 1536 | bytes 6144 | tf_op jit(solution)/shard_map/psum | solution.py:325
  494.9 87.6 %all-reduce.20.cloned.1.call-done = (bf16[320,1024]{1,0:T(8,128)(2,1)}, bf16[320,256]{1,0:T(8,128)(2,1)}, bf16[320,256]{1,0:T(8,128)(2,1)}, bf16[512,640]{1,0:T(...) async-done(((bf16[320,1024]{1,0:T(8,128)(2,1)}, bf16[320,256]{1,0:T(8,128)(2,1)}, bf16[320,256]{1,0:T(8,128)(2,1)}, ...) | async-done | bytes 5570576 | tf_op jit(solution)/shard_map/psum | solution.py:321
  582.5 2.4 convert_element_type.252
  (260 shorter events, 76.7 us)
Async XLA Ops:
  7.2 20.8 %copy-start = (bf16[256,640]{1,0:T(8,128)(2,1)S(1)}, bf16[256,640]{1,0:T(8,128)(2,1)}, u32[]{:S(2)}) copy-start(bf16[256,640]{1,0:T(8,128)(2,1)} %param.16) | copy-start | bytes 983044
  7.3 60.6 %all-gather.8.cloned.1.call-start = ((), (), s32[]{:S(2)}) async-start(), calls=%async_computation.7 | async-start | bytes 1966080 | tf_op jit(solution)/shard_map/all_gather | solution.py:94
  8.0 26.9 %copy-start.48 = (s32[256]{0:T(256)S(1)}, s32[256]{0:T(256)}, u32[]{:S(2)}) copy-start(s32[256]{0:T(256)} %param.17) | copy-start | bytes 3076
  8.0 32.8 %copy-start.55 = (bf16[128]{0:T(256)(128)(2,1)S(1)}, bf16[128]{0:T(256)(128)(2,1)}, u32[]{:S(2)}) copy-start(bf16[128]{0:T(256)(128)(2,1)} %param.30) | copy-start | bytes 772
  8.0 37.0 %copy-start.41 = (bf16[320,256]{1,0:T(8,128)(2,1)S(1)}, bf16[320,256]{1,0:T(8,128)(2,1)}, u32[]{:S(2)}) copy-start(bf16[320,256]{1,0:T(8,128)(2,1)} %param.19) | copy-start | bytes 491524
  8.0 67.9 %all-gather.10.cloned.1.call-start = ((), (), s32[]{:S(2)}) async-start(), calls=%async_computation.8 | async-start | bytes 1966080 | tf_op jit(solution)/shard_map/all_gather | solution.py:97
  8.8 103.4 %all-gather.12.cloned.1.call-start = ((), (), s32[]{:S(2)}) async-start(), calls=%async_computation.9 | async-start | bytes 3932160 | tf_op jit(solution)/shard_map/all_gather | solution.py:98
  9.5 143.0 %all-gather.14.cloned.1.call-start = ((), (), s32[]{:S(2)}) async-start(), calls=%async_computation.10 | async-start | bytes 3932160 | tf_op jit(solution)/shard_map/all_gather | solution.py:99
  10.1 182.9 %all-gather.16.cloned.1.call-start = ((), (), s32[]{:S(2)}) async-start(), calls=%async_computation.11 | async-start | bytes 3932160 | tf_op jit(solution)/shard_map/all_gather | solution.py:100
  28.8 30.9 %copy-start.56 = (bf16[128]{0:T(256)(128)(2,1)S(1)}, bf16[128]{0:T(256)(128)(2,1)}, u32[]{:S(2)}) copy-start(bf16[128]{0:T(256)(128)(2,1)} %param.29) | copy-start | bytes 772
  29.1 44.9 %copy-start.42 = (bf16[256,256]{1,0:T(8,128)(2,1)}, bf16[256,256]{1,0:T(8,128)(2,1)S(1)}, u32[]{:S(2)}) copy-start(bf16[256,256]{1,0:T(8,128)(2,1)S(1)} %convolution_convert_fusion.9) | copy-start | bytes 393220
  29.1 44.8 %collective-permute-start.1 = (bf16[256,256]{1,0:T(8,128)(2,1)S(1)}, bf16[256,256]{1,0:T(8,128)(2,1)S(1)}, u32[]{:S(2)}, u32[]{:S(2)}) collective-permute-start(bf16[256,256]{1,0:T(8,128)(2,1)S(1)} %convolution_convert_fusion.9), channel_id=1, source_target_pairs={{0,1},{1,2},{2,3},{3,4},{4,5},{5,6},{6,7},{7,8},{8,9},{9,10},{10,1... | collective-permute-start | bytes 393224 | tf_op jit(solution)/shard_map/ppermute | solution.py:17
  33.5 40.4 %collective-permute-start = (bf16[256,256]{1,0:T(8,128)(2,1)S(1)}, bf16[256,256]{1,0:T(8,128)(2,1)S(1)}, u32[]{:S(2)}, u32[]{:S(2)}) collective-permute-start(bf16[256,256]{1,0:T(8,128)(2,1)S(1)} %convolution_convert_fusion.9), channel_id=1, source_target_pairs={{0,2},{1,3},{2,4},{3,5},{4,6},{5,7},{6,8},{7,9},{8,10},{9,11},{10,... | collective-permute-start | bytes 393224 | tf_op jit(solution)/shard_map/ppermute | solution.py:17
  34.9 30.2 %collective-permute-start.3 = (s32[256]{0:T(256)S(1)}, s32[256]{0:T(256)S(1)}, u32[]{:S(2)}, u32[]{:S(2)}) collective-permute-start(s32[256]{0:T(256)S(1)} %copy-done.48), channel_id=1, source_target_pairs={{0,1},{1,2},{2,3},{3,4},{4,5},{5,6},{6,7},{7,8},{8,9},{9,10},{10,1... | collective-permute-start | bytes 3080 | tf_op jit(solution)/shard_map/ppermute | solution.py:17
  38.0 29.0 %collective-permute-start.2 = (s32[256]{0:T(256)S(1)}, s32[256]{0:T(256)S(1)}, u32[]{:S(2)}, u32[]{:S(2)}) collective-permute-start(s32[256]{0:T(256)S(1)} %copy-done.48), channel_id=1, source_target_pairs={{0,2},{1,3},{2,4},{3,5},{4,6},{5,7},{6,8},{7,9},{8,10},{9,11},{10,... | collective-permute-start | bytes 3080 | tf_op jit(solution)/shard_map/ppermute | solution.py:17
  54.7 16.5 %collective-permute-start.5 = (bf16[256,256]{0,1:T(8,128)(2,1)}, bf16[256,256]{0,1:T(8,128)(2,1)}, u32[]{:S(2)}, u32[]{:S(2)}) collective-permute-start(bf16[256,256]{0,1:T(8,128)(2,1)} %maximum_bitcast_fusion.6), channel_id=1, source_target_pairs={{0,1},{1,2},{2,3},{3,4},{4,5},{5,6},{6,7},{7,8},{8,9},{9,10},{10,1... | collective-permute-start | bytes 393224 | tf_op jit(solution)/shard_map/ppermute | solution.py:17
  59.0 202.7 %reduce-scatter.10.cloned.1.call-start = ((), (), s32[]{:S(2)}) async-start(), calls=%async_computation.13 | async-start | bytes 491520 | tf_op jit(solution)/shard_map/reduce_scatter | solution.py:298
  59.6 11.4 %copy-start.26 = (f32[256,128]{1,0:T(8,128)}, f32[256,128]{1,0:T(8,128)S(1)}, u32[]{:S(2)}) copy-start(f32[256,128]{1,0:T(8,128)S(1)} %get-tuple-element.70) | copy-start | bytes 393220
  65.1 6.1 %collective-permute-start.4 = (bf16[256,256]{0,1:T(8,128)(2,1)}, bf16[256,256]{0,1:T(8,128)(2,1)}, u32[]{:S(2)}, u32[]{:S(2)}) collective-permute-start(bf16[256,256]{0,1:T(8,128)(2,1)} %maximum_bitcast_fusion.6), channel_id=1, source_target_pairs={{0,2},{1,3},{2,4},{3,5},{4,6},{5,7},{6,8},{7,9},{8,10},{9,11},{10,... | collective-permute-start | bytes 393224 | tf_op jit(solution)/shard_map/ppermute | solution.py:17
  157.8 38.5 %copy-start.9 = (bf16[256,640]{1,0:T(8,128)(2,1)S(1)}, bf16[256,640]{1,0:T(8,128)(2,1)}, u32[]{:S(2)}) copy-start(bf16[256,640]{1,0:T(8,128)(2,1)} %param.31) | copy-start | bytes 983044
  220.1 16.6 %collective-permute-start.7 = (bf16[256,256]{0,1:T(8,128)(2,1)}, bf16[256,256]{0,1:T(8,128)(2,1)}, u32[]{:S(2)}, u32[]{:S(2)}) collective-permute-start(bf16[256,256]{0,1:T(8,128)(2,1)} %get-tuple-element.64), channel_id=1, source_target_pairs={{1,0},{2,1},{3,2},{4,3},{5,4},{6,5},{7,6},{8,7},{9,8},{10,9},{11,1... | collective-permute-start | bytes 393224 | tf_op jit(solution)/shard_map/ppermute | solution.py:17
  221.4 15.3 %collective-permute-start.6 = (bf16[256,256]{0,1:T(8,128)(2,1)}, bf16[256,256]{0,1:T(8,128)(2,1)}, u32[]{:S(2)}, u32[]{:S(2)}) collective-permute-start(bf16[256,256]{0,1:T(8,128)(2,1)} %get-tuple-element.63), channel_id=1, source_target_pairs={{2,0},{3,1},{4,2},{5,3},{6,4},{7,5},{8,6},{9,7},{10,8},{11,9},{12,... | collective-permute-start | bytes 393224 | tf_op jit(solution)/shard_map/ppermute | solution.py:17
  234.1 8.7 %collective-permute-start.9 = (bf16[256,256]{1,0:T(8,128)(2,1)}, bf16[256,256]{1,0:T(8,128)(2,1)S(1)}, u32[]{:S(2)}, u32[]{:S(2)}) collective-permute-start(bf16[256,256]{1,0:T(8,128)(2,1)} %get-tuple-element.62), channel_id=1, source_target_pairs={{1,0},{2,1},{3,2},{4,3},{5,4},{6,5},{7,6},{8,7},{9,8},{10,9},{11,1... | collective-permute-start | bytes 393224 | tf_op jit(solution)/shard_map/ppermute | solution.py:17
  235.4 7.4 %collective-permute-start.8 = (bf16[256,256]{1,0:T(8,128)(2,1)S(1)}, bf16[256,256]{1,0:T(8,128)(2,1)S(1)}, u32[]{:S(2)}, u32[]{:S(2)}) collective-permute-start(bf16[256,256]{1,0:T(8,128)(2,1)S(1)} %get-tuple-element.61), channel_id=1, source_target_pairs={{2,0},{3,1},{4,2},{5,3},{6,4},{7,5},{8,6},{9,7},{10,8},{11,9},{12,... | collective-permute-start | bytes 393224 | tf_op jit(solution)/shard_map/ppermute | solution.py:17
  240.5 32.6 %reduce-scatter.12.cloned.1.call-start = ((), (), s32[]{:S(2)}) async-start(), calls=%async_computation.14 | async-start | bytes 491520 | tf_op jit(solution)/shard_map/reduce_scatter | solution.py:301
  245.5 53.6 %reduce-scatter.8.cloned.1.call-start = ((), (), s32[]{:S(2)}) async-start(), calls=%async_computation.12 | async-start | bytes 1966080 | tf_op jit(solution)/shard_map/reduce_scatter | solution.py:295
  250.1 75.3 %reduce-scatter.14.cloned.1.call-start = ((), (), s32[]{:S(2)}) async-start(), calls=%async_computation.15 | async-start | bytes 1966080 | tf_op jit(solution)/shard_map/reduce_scatter | solution.py:304
  251.8 113.9 %reduce-scatter.16.cloned.1.call-start = ((), (), s32[]{:S(2)}) async-start(), calls=%async_computation.16 | async-start | bytes 3932160 | tf_op jit(solution)/shard_map/reduce_scatter | solution.py:186
  254.2 152.0 %reduce-scatter.18.cloned.1.call-start = ((), (), s32[]{:S(2)}) async-start(), calls=%async_computation.17 | async-start | bytes 3932160 | tf_op jit(solution)/shard_map/reduce_scatter | solution.py:189
  257.8 188.8 %reduce-scatter.20.cloned.1.call-start = ((), (), s32[]{:S(2)}) async-start(), calls=%async_computation.18 | async-start | bytes 3932160 | tf_op jit(solution)/shard_map/reduce_scatter | solution.py:192
  261.7 320.8 %all-reduce.20.cloned.1.call-start = ((), (), s32[]{:S(2)}) async-start(), calls=%async_computation.19 | async-start | bytes 11141120 | tf_op jit(solution)/shard_map/psum | solution.py:321
  448.4 45.4 %copy-start.2 = (f32[256,640]{1,0:T(8,128)S(1)}, f32[256,640]{1,0:T(8,128)}, u32[]{:S(2)}) copy-start(f32[256,640]{1,0:T(8,128)} %copy-done.1) | copy-start | bytes 1966084
  (49 other events, 144.7 us)
Sparse Core Ops, SparseCore 0:
  9.6 30.6 all-gather.7
  41.9 28.2 all-gather.9
  71.7 40.3 all-gather.11
  113.5 38.9 all-gather.13
  153.9 38.9 all-gather.15
  240.6 17.6 reduce-scatter.9
  260.5 12.4 reduce-scatter.11
  275.9 23.2 reduce-scatter.7
  302.0 23.2 reduce-scatter.13
  328.0 37.6 reduce-scatter.15
  368.5 37.6 reduce-scatter.17
  408.9 37.6 reduce-scatter.19
  451.3 131.1 all-reduce.19
where the time goes:
time: 602 us; the launch traced here: 601 us
  waiting for transfers between devices  382 us (63%)
  blocking collectives  72.1 us (12%)
  matrix products  61.4 us (10%)
  other arithmetic  29.2 us (5%)
  starting transfers between devices  23.9 us (4%)
  between operations  17 us (3%)
  local copies, waits for them, and re-layouts  15.4 us (3%)
    psum x1, waiting for transfers between devices, per_device(): lax.psum(attn_parts[0].astype(jnp.bfloat16), 'seq').astype(jnp.float32)  87.6 us
    reduce_scatter x1, waiting for transfers between devices, per_device(): lax.psum_scatter(ff_gradients[1].astype(jnp.bfloat16), 'wshard', scatter_...  40.5 us
    reduce_scatter x1, waiting for transfers between devices, per_device(): lax.psum_scatter(ff_gradients[2].astype(jnp.bfloat16), 'wshard', scatter_...  40.4 us
    reduce_scatter x1, waiting for transfers between devices, per_device(): lax.psum_scatter(ff_gradients[0].astype(jnp.bfloat16), 'wshard', scatter_...  40.4 us
    all_gather x1, waiting for transfers between devices, per_device(): lax.all_gather(w_up, 'wshard', axis=0, tiled=True)  36.4 us
    all_gather x1, waiting for transfers between devices, per_device(): lax.all_gather(w_down, 'wshard', axis=0, tiled=True)  35.2 us
    psum x1, blocking collectives, per_device(): lax.psum(attn_parts[4].astype(jnp.bfloat16), 'seq').astype(jnp.float32)  34.5 us
    all_gather x1, waiting for transfers between devices, per_device(): lax.all_gather(w_gate, 'wshard', axis=0, tiled=True)  33.6 us
  transfers between devices with their start and end apart: 23, of which 11 were waited for; matrix products, arithmetic and copies ran while one was open for 10% of the time, Pallas kernels for 0%

commit v1 on v0

--- a/solution.py
+++ b/solution.py
@@ -1,6 +1,10 @@
+import functools
+
 import jax
 import jax.numpy as jnp
 from jax import lax
+from jax.experimental import pallas as pl
+from jax.experimental.pallas import tpu as pltpu
 from jax.sharding import PartitionSpec as P
 
 WINDOW = 512
@@ -72,7 +76,546 @@
     return jnp.einsum("tc,tf->cf", left_rows, right_rows, preferred_element_type=jnp.float32)
 
 
+MESH = pl.DeviceIdType.MESH
+LANES = 128
+
+
+def coordinates():
+    seq = lax.axis_index("seq")
+    return lax.rem(seq // 2, 2), lax.rem(seq, 2), seq // 4, lax.axis_index("wshard")
+
+
+def device(x, core, z, y):
+    return ((z * 2 + x) * 2 + core, y)
+
+
+def greet(partners):
+    barrier = pltpu.get_barrier_semaphore()
+    for partner in partners:
+        pl.semaphore_signal(barrier, inc=1, device_id=partner, device_id_type=MESH)
+    pl.semaphore_wait(barrier, len(partners))
+
+
+def remote(src, dst, send, recv, target):
+    return pltpu.make_async_remote_copy(
+        src_ref=src, dst_ref=dst, send_sem=send, recv_sem=recv,
+        device_id=target, device_id_type=MESH,
+    )
+
+
+def gather_kernel(count, *refs):
+    shards, fulls = refs[:count], refs[count : 2 * count]
+    own_sem, send_sems, recv_sems = refs[2 * count :]
+    x, core, z, y = coordinates()
+    sibling = device(x, 1 - core, z, y)
+    beside = device(1 - x, core, z, y)
+    across = device(x, core, z, 1 - y)
+    greet([sibling, beside, across])
+
+    def local(i):
+        rows = shards[i].shape[0]
+        return pltpu.make_async_copy(
+            shards[i], fulls[i].at[pl.ds(y * rows, rows)], own_sem.at[i]
+        )
+
+    def first(i):
+        rows = shards[i].shape[0]
+        part = rows if i == count - 1 else rows // 4
+        at = 0 if i == count - 1 else (core * 2 + x) * part
+        return remote(
+            shards[i].at[pl.ds(at, part)], fulls[i].at[pl.ds(y * rows + at, part)],
+            send_sems.at[0, i], recv_sems.at[0, i], across,
+        )
+
+    def second(i):
+        rows = shards[i].shape[0]
+        part = rows // 4
+        block = fulls[i].at[pl.ds((1 - y) * rows + (core * 2 + x) * part, part)]
+        return remote(block, block, send_sems.at[1, i], recv_sems.at[1, i], beside)
+
+    def third(i):
+        rows = shards[i].shape[0]
+        part = rows // 2
+        block = fulls[i].at[pl.ds((1 - y) * rows + core * part, part)]
+        return remote(block, block, send_sems.at[2, i], recv_sems.at[2, i], sibling)
+
+    order = [count - 1] + list(range(count - 1))
+    for i in order:
+        first(i).start()
+    for i in range(count):
+        local(i).start()
+    first(count - 1).wait_recv()
+    big = count - 1
+    for step in range(big + 1):
+        if step < big:
+            first(step).wait_recv()
+            second(step).start()
+        if step >= 1:
+            second(step - 1).wait_recv()
+            third(step - 1).start()
+    for i in range(big):
+        third(i).wait_recv()
+    for i in range(count):
+        local(i).wait()
+        first(i).wait_send()
+    for i in range(big):
+        second(i).wait_send()
+        third(i).wait_send()
+
+
+def gather_weights(shards):
+    count = len(shards)
+    return pl.pallas_call(
+        functools.partial(gather_kernel, count),
+        out_shape=[jax.ShapeDtypeStruct((2 * s.shape[0],) + s.shape[1:], s.dtype) for s in shards],
+        in_specs=[pl.BlockSpec(memory_space=pl.ANY)] * count,
+        out_specs=[pl.BlockSpec(memory_space=pltpu.VMEM)] * count,
+        scratch_shapes=[
+            pltpu.SemaphoreType.DMA((count,)),
+            pltpu.SemaphoreType.DMA((3, count)),
+            pltpu.SemaphoreType.DMA((3, count)),
+        ],
+        compiler_params=pltpu.CompilerParams(
+            collective_id=1, has_side_effects=True, vmem_limit_bytes=48 * 2**20
+        ),
+        name="gather_weights",
+    )(*shards)
+
+
+def reduce_kernel(
+    terms, gains, out, gains_out,
+    from_core, from_across, from_beside, from_line, gain_in,
+    send_core, recv_core, send_across, recv_across, send_beside, recv_beside,
+    send_line, recv_line, send_zline, recv_zline, send_xback, recv_xback,
+    send_back, recv_back, send_gain, recv_gain,
+):
+    chunks = terms.shape[0]
+    depth = terms.shape[4]
+    x, core, z, y = coordinates()
+    sibling = device(x, 1 - core, z, y)
+    beside = device(1 - x, core, z, y)
+    across = device(x, core, z, 1 - y)
+    line = [device(x, core, lax.rem(z + d, depth), y) for d in range(1, depth)]
+    greet([sibling, beside, across] + line)
+
+    def to_core(c):
+        return remote(terms.at[c, 1 - core], from_core.at[c], send_core.at[c], recv_core.at[c], sibling)
+
+    def to_across(c):
+        return remote(
+            from_core.at[c, 1 - y], from_across.at[c], send_across.at[c], recv_across.at[c], across
+        )
+
+    def to_beside(c):
+        return remote(
+            from_across.at[c, 1 - x], from_beside.at[c], send_beside.at[c], recv_beside.at[c], beside
+        )
+
+    def to_line(c, d):
+        return remote(
+            from_beside.at[c, lax.rem(z + d, depth)], from_line.at[c, d - 1],
+            send_line.at[c, d - 1], recv_line.at[c, d - 1], line[d - 1],
+        )
+
+    def along_line(c, d):
+        block = out.at[c, core, x, z]
+        return remote(block, block, send_zline.at[c, d - 1], recv_zline.at[c, d - 1], line[d - 1])
+
+    def along_line_arrival(c, d):
+        block = out.at[c, core, x, lax.rem(z + depth - d, depth)]
+        return remote(block, block, send_zline.at[c, d - 1], recv_zline.at[c, d - 1], line[d - 1])
+
+    def back_beside(c, side):
+        block = out.at[c, core, side]
+        return remote(block, block, send_xback.at[c], recv_xback.at[c], beside)
+
+    def back_core(c, side):
+        block = out.at[c, side]
+        return remote(block, block, send_back.at[c], recv_back.at[c], sibling)
+
+    def gain_copy(step):
+        target = ([sibling, across, beside] + line)[step]
+        src = gains if step == 0 else gains_out.at[min(step, 3) - 1]
+        return remote(src, gain_in.at[step], send_gain.at[step], recv_gain.at[step], target)
+
+    def add(a, b):
+        return (a.astype(jnp.float32) + b.astype(jnp.float32)).astype(jnp.bfloat16)
+
+    @pl.loop(0, chunks)
+    def _(c):
+        to_core(c).start()
+
+    gain_copy(0).start()
+
+    def stage(at, action):
+        @pl.when((at >= 0) & (at < chunks))
+        def _():
+            action(at)
+
+    def after_core(c):
+        to_core(c).wait_recv()
+        from_core[c, 1 - y] = add(from_core[c, 1 - y], terms[c, core, 1 - y])
+        to_across(c).start()
+        from_core[c, y] = add(from_core[c, y], terms[c, core, y])
+
+    def after_across(c):
+        to_across(c).wait_recv()
+        from_across[c, 1 - x] = add(from_across[c, 1 - x], from_core[c, y, 1 - x])
+        to_beside(c).start()
+        from_across[c, x] = add(from_across[c, x], from_core[c, y, x])
+
+    def after_beside(c):
+        to_beside(c).wait_recv()
+        from_beside[c] = add(from_beside[c], from_across[c, x])
+        for d in range(1, depth):
+            to_line(c, d).start()
+
+    def after_line(c):
+        total = from_beside[c, z].astype(jnp.float32)
+        for d in range(1, depth):
+            to_line(c, d).wait_recv()
+            total = total + from_line[c, d - 1].astype(jnp.float32)
+        out[c, core, x, z] = total.astype(jnp.bfloat16)
+        for d in range(1, depth):
+            along_line(c, d).start()
+
+    def after_zline(c):
+        for d in range(1, depth):
+            along_line_arrival(c, d).wait_recv()
+        back_beside(c, x).start()
+
+    def after_xback(c):
+        back_beside(c, 1 - x).wait_recv()
+        back_core(c, core).start()
+
+    actions = [after_core, after_across, after_beside, after_line, after_zline, after_xback]
+
+    @pl.loop(0, chunks + len(actions) - 1)
+    def _(t):
+        for lag, action in enumerate(actions):
+            stage(t - lag, action)
+        for step in range(3):
+            @pl.when(t == step + 1)
+            def _():
+                gain_copy(step).wait_recv()
+                before = gains[...] if step == 0 else gains_out[step - 1]
+                gains_out[step] = before + gain_in[step]
+                if step < 2:
+                    gain_copy(step + 1).start()
+                else:
+                    for d in range(1, depth):
+                        gain_copy(2 + d).start()
+
+    total = gains_out[2]
+    for d in range(1, depth):
+        gain_copy(2 + d).wait_recv()
+        total = total + gain_in[2 + d]
+    gains_out[3] = total
+    for step in range(2 + depth):
+        gain_copy(step).wait_send()
+
+    @pl.loop(0, chunks)
+    def _(c):
+        back_core(c, 1 - core).wait_recv()
+        to_core(c).wait_send()
+        to_across(c).wait_send()
+        to_beside(c).wait_send()
+        for d in range(1, depth):
+            to_line(c, d).wait_send()
+            along_line(c, d).wait_send()
+        back_beside(c, x).wait_send()
+        back_core(c, core).wait_send()
+
+
+def reduce_terms(terms, gains):
+    chunks, _, _, _, depth, rows, lanes = terms.shape
+    piece = (rows, lanes)
+    dma = pltpu.SemaphoreType.DMA
+    vmem = pl.BlockSpec(memory_space=pltpu.VMEM)
+    pair = [dma((chunks,)), dma((chunks,))]
+    lines = [dma((chunks, depth - 1)), dma((chunks, depth - 1))]
+    steps = 2 + depth
+    return pl.pallas_call(
+        reduce_kernel,
+        out_shape=[
+            jax.ShapeDtypeStruct((chunks, 2, 2, depth) + piece, jnp.bfloat16),
+            jax.ShapeDtypeStruct((4,) + gains.shape, jnp.float32),
+        ],
+        in_specs=[vmem, vmem],
+        out_specs=[vmem, vmem],
+        scratch_shapes=[
+            pltpu.VMEM((chunks, 2, 2, depth) + piece, jnp.bfloat16),
+            pltpu.VMEM((chunks, 2, depth) + piece, jnp.bfloat16),
+            pltpu.VMEM((chunks, depth) + piece, jnp.bfloat16),
+            pltpu.VMEM((chunks, depth - 1) + piece, jnp.bfloat16),
+            pltpu.VMEM((steps,) + gains.shape, jnp.float32),
+        ]
+        + pair + pair + pair + lines + lines + pair + pair
+        + [dma((steps,)), dma((steps,))],
+        compiler_params=pltpu.CompilerParams(
+            collective_id=2, has_side_effects=True, vmem_limit_bytes=48 * 2**20
+        ),
+        name="reduce_terms",
+    )(terms, gains)
+
+
+def split_columns(term, depth):
+    rows, columns = term.shape
+    term = term.reshape(2, 2, 2, rows // 8, columns // (depth * LANES), depth, LANES)
+    return term.transpose(4, 1, 0, 2, 5, 3, 6)
+
+
+def join_columns(pieces):
+    chunks, _, _, depth, rows, lanes = pieces.shape
+    return pieces.transpose(1, 2, 4, 0, 3, 5).reshape(4 * rows, chunks * depth * lanes)
+
+
+def split_rows(term, depth, piece_rows):
+    rows, columns = term.shape
+    tiles = columns // LANES
+    high = piece_rows // tiles
+    chunks = rows // (8 * depth * high)
+    term = term.reshape(2, chunks, 2, 2, depth, high, tiles, LANES)
+    term = term.transpose(1, 2, 0, 3, 4, 6, 5, 7)
+    return term.reshape(chunks, 2, 2, 2, depth, tiles * high, LANES)
+
+
+def join_rows(pieces, columns):
+    chunks, _, _, depth, piece_rows, lanes = pieces.shape
+    tiles = columns // lanes
+    high = piece_rows // tiles
+    pieces = pieces.reshape(chunks, 2, 2, depth, tiles, high, lanes).transpose(0, 1, 2, 3, 5, 4, 6)
+    return pieces.reshape(chunks * 4 * depth * high, columns)
+
+
 def per_device(
+    inputs,
+    doc_ids,
+    w_query,
+    w_key,
+    w_value,
+    w_out,
+    w_gate,
+    w_up,
+    w_down,
+    gain_in,
+    gain_attn_post,
+    gain_ff_pre,
+    gain_ff_post,
+    gain_query,
+    gain_key,
+    cotangent,
+):
+    small = (gain_in, gain_attn_post, gain_ff_pre, gain_ff_post, gain_query, gain_key)
+    small_shard = jnp.concatenate(small).astype(jnp.float32).reshape(1, -1, LANES)
+    gathered = gather_weights(
+        (w_query, w_key, w_value, w_out, w_gate, w_up, w_down, small_shard)
+    )
+    full_query, full_key, full_value, full_out, full_gate, full_up, full_down = gathered[:7]
+    small_full = gathered[7].reshape(2, -1)
+    starts = [0]
+    for vec in small:
+        starts.append(starts[-1] + vec.shape[0])
+    in_gain, attn_post_gain, ff_pre_gain, ff_post_gain, query_gain, key_gain = [
+        small_full[:, low:high].reshape(-1) for low, high in zip(starts[:-1], starts[1:])
+    ]
+    row_count = inputs.shape[0]
+    head_dim = full_key.shape[1]
+    head_count = full_query.shape[1] // head_dim
+    score_scale = head_dim ** (-0.5)
+    start_row = lax.axis_index(("seq", "wshard")) * row_count
+    query_pos = start_row + jnp.arange(row_count, dtype=jnp.int32)
+    cos_table, sin_table = rope_tables(query_pos, head_dim)
+    x_float = inputs.astype(jnp.float32)
+    normed_in = rms_gain(x_float, in_gain).astype(jnp.bfloat16)
+    query_raw = jnp.dot(normed_in, full_query, preferred_element_type=jnp.float32).reshape(
+        row_count, head_count, head_dim
+    )
+    key_raw = jnp.dot(normed_in, full_key, preferred_element_type=jnp.float32)[:, None, :]
+    values = jnp.dot(normed_in, full_value, preferred_element_type=jnp.float32).astype(jnp.bfloat16)
+    queries = norm_rope(query_raw, query_gain, cos_table, sin_table).astype(jnp.bfloat16)
+    key_rot = norm_rope(key_raw, key_gain, cos_table, sin_table)[:, 0].astype(jnp.bfloat16)
+    sent_rows = min(WINDOW, row_count)
+    hop_count = WINDOW // sent_rows
+    outgoing = (key_rot, values, doc_ids)
+    halo_keys = []
+    halo_values = []
+    halo_docs = []
+    for distance in range(hop_count, 0, -1):
+        arrived = from_behind((outgoing[0], outgoing[1], outgoing[2]), ("seq", "wshard"), distance)
+        halo_keys.append(arrived[0])
+        halo_values.append(arrived[1])
+        halo_docs.append(arrived[2])
+    all_keys = jnp.concatenate(halo_keys + [key_rot], 0)
+    all_values = jnp.concatenate(halo_values + [values], 0)
+    all_docs = jnp.concatenate(halo_docs + [doc_ids], 0)
+    key_pos = start_row - WINDOW + jnp.arange(WINDOW + row_count, dtype=jnp.int32)
+    allowed = window_mask(query_pos, key_pos, doc_ids, all_docs)
+    scores = masked_scores(queries, all_keys, allowed, score_scale)
+    row_peak = jnp.max(scores, axis=-1, keepdims=True)
+    row_total = jnp.sum(
+        jnp.where(allowed[None], jnp.exp(scores - row_peak), 0.0), axis=-1, keepdims=True
+    )
+    log_total = row_peak + jnp.log(row_total)
+    soft = jnp.where(allowed[None], jnp.exp(scores - log_total), 0.0).astype(jnp.bfloat16)
+    attended = jnp.einsum("hqk,kd->qhd", soft, all_values, preferred_element_type=jnp.float32)
+    attended = attended.reshape(row_count, head_count * head_dim).astype(jnp.bfloat16)
+    attn_proj = jnp.dot(attended, full_out, preferred_element_type=jnp.float32)
+    resid = x_float + rms_gain(attn_proj, attn_post_gain)
+    normed_ff = rms_gain(resid, ff_pre_gain).astype(jnp.bfloat16)
+    gate_pre = jnp.dot(normed_ff, full_gate, preferred_element_type=jnp.float32)
+    up_pre = jnp.dot(normed_ff, full_up, preferred_element_type=jnp.float32)
+    hidden = geglu(gate_pre, up_pre).astype(jnp.bfloat16)
+    ff_proj = jnp.dot(hidden, full_down, preferred_element_type=jnp.float32)
+    layer_out = (resid + rms_gain(ff_proj, ff_post_gain)).astype(jnp.bfloat16)
+    grad_top = cotangent.astype(jnp.float32)
+    _, pullback = jax.vjp(rms_gain, ff_proj, ff_post_gain)
+    grad_ff_proj, grad_gain_ff_post = pullback(grad_top)
+    grad_ff_proj = grad_ff_proj.astype(jnp.bfloat16)
+    grad_w_down = weight_grad(hidden, grad_ff_proj)
+    grad_hidden = lax.dot_general(
+        grad_ff_proj, full_down, (((1,), (1,)), ((), ())), preferred_element_type=jnp.float32
+    )
+    _, pullback = jax.vjp(geglu, gate_pre, up_pre)
+    grad_gate, grad_up = pullback(grad_hidden)
+    grad_gate = grad_gate.astype(jnp.bfloat16)
+    grad_up = grad_up.astype(jnp.bfloat16)
+    grad_w_gate = weight_grad(normed_ff, grad_gate)
+    grad_w_up = weight_grad(normed_ff, grad_up)
+    grad_normed_ff = lax.dot_general(
+        grad_gate, full_gate, (((1,), (1,)), ((), ())), preferred_element_type=jnp.float32
+    )
+    grad_normed_ff = grad_normed_ff + lax.dot_general(
+        grad_up, full_up, (((1,), (1,)), ((), ())), preferred_element_type=jnp.float32
+    )
+    _, pullback = jax.vjp(rms_gain, resid, ff_pre_gain)
+    grad_resid_part, grad_gain_ff_pre = pullback(grad_normed_ff)
+    grad_resid = grad_top + grad_resid_part
+    ff_gradients = (grad_w_gate, grad_w_up, grad_w_down, grad_gain_ff_pre, grad_gain_ff_post)
+    _, pullback = jax.vjp(rms_gain, attn_proj, attn_post_gain)
+    grad_attn_proj, grad_gain_attn_post = pullback(grad_resid)
+    grad_attn_proj = grad_attn_proj.astype(jnp.bfloat16)
+    grad_w_out = weight_grad(attended, grad_attn_proj)
+    grad_attended = lax.dot_general(
+        grad_attn_proj, full_out, (((1,), (1,)), ((), ())), preferred_element_type=jnp.float32
+    ).astype(jnp.bfloat16)
+    grad_heads = grad_attended.reshape(row_count, head_count, head_dim)
+    again_scores = masked_scores(queries, all_keys, allowed, score_scale)
+    probs = jnp.where(allowed[None], jnp.exp(again_scores - log_total), 0.0)
+    grad_soft = jnp.einsum(
+        "qhd,kd->hqk", grad_heads, all_values, preferred_element_type=jnp.float32
+    )
+    row_inner = jnp.sum(probs * grad_soft, axis=-1, keepdims=True)
+    grad_score = (probs * (grad_soft - row_inner) * score_scale).astype(jnp.bfloat16)
+    grad_queries = jnp.einsum(
+        "hqk,kd->qhd", grad_score, all_keys, preferred_element_type=jnp.float32
+    )
+    grad_keys_all = jnp.einsum(
+        "hqk,qhd->kd", grad_score, queries, preferred_element_type=jnp.float32
+    )
+    grad_values_all = jnp.einsum(
+        "hqk,qhd->kd", probs.astype(jnp.bfloat16), grad_heads, preferred_element_type=jnp.float32
+    )
+    back_keys = jnp.zeros((sent_rows, head_dim), jnp.float32)
+    back_values = jnp.zeros((sent_rows, head_dim), jnp.float32)
+    for piece_index in range(hop_count):
+        distance = hop_count - piece_index
+        piece_start = piece_index * sent_rows
+        arrived = (
+            from_behind(
+                grad_keys_all[piece_start : piece_start + sent_rows].astype(jnp.bfloat16),
+                ("seq", "wshard"),
+                -distance,
+            ).astype(jnp.float32),
+            from_behind(
+                grad_values_all[piece_start : piece_start + sent_rows].astype(jnp.bfloat16),
+                ("seq", "wshard"),
+                -distance,
+            ).astype(jnp.float32),
+        )
+        back_keys = back_keys + arrived[0]
+        back_values = back_values + arrived[1]
+    own_keys = grad_keys_all[WINDOW:]
+    own_values = grad_values_all[WINDOW:]
+    split_row = row_count - sent_rows
+    grad_keys = jnp.concatenate([own_keys[:split_row], own_keys + back_keys], 0)
+    grad_values = jnp.concatenate([own_values[:split_row], own_values + back_values], 0).astype(
+        jnp.bfloat16
+    )
+
+    def query_path(tensor, gain_vec):
+        return norm_rope(tensor, gain_vec, cos_table, sin_table)
+
+    _, pullback = jax.vjp(query_path, query_raw, query_gain)
+    grad_query_raw, grad_gain_query = pullback(grad_queries)
+    _, pullback = jax.vjp(query_path, key_raw, key_gain)
+    grad_key_raw, grad_gain_key = pullback(grad_keys[:, None, :])
+    grad_query_raw = grad_query_raw.reshape(row_count, head_count * head_dim).astype(jnp.bfloat16)
+    grad_key_raw = grad_key_raw[:, 0].astype(jnp.bfloat16)
+    grad_w_query = weight_grad(normed_in, grad_query_raw)
+    grad_w_key = weight_grad(normed_in, grad_key_raw)
+    grad_w_value = weight_grad(normed_in, grad_values)
+    grad_normed_in = lax.dot_general(
+        grad_query_raw, full_query, (((1,), (1,)), ((), ())), preferred_element_type=jnp.float32
+    )
+    grad_normed_in = grad_normed_in + lax.dot_general(
+        grad_key_raw, full_key, (((1,), (1,)), ((), ())), preferred_element_type=jnp.float32
+    )
+    grad_normed_in = grad_normed_in + lax.dot_general(
+        grad_values, full_value, (((1,), (1,)), ((), ())), preferred_element_type=jnp.float32
+    )
+    _, pullback = jax.vjp(rms_gain, x_float, in_gain)
+    grad_input_part, grad_gain_in = pullback(grad_normed_in)
+    grad_inputs = grad_resid + grad_input_part
+    attn_gradients = (
+        grad_w_query,
+        grad_w_key,
+        grad_w_value,
+        grad_w_out,
+        grad_gain_in,
+        grad_gain_attn_post,
+        grad_gain_query,
+        grad_gain_key,
+    )
+    depth = lax.axis_size("seq") // 4
+    bf16 = [g.astype(jnp.bfloat16) for g in attn_gradients[:4] + ff_gradients[:3]]
+    by_columns = [
+        bf16[4], bf16[5], bf16[0], jnp.concatenate([bf16[1], bf16[2]], axis=1)
+    ]
+    pieces = [split_columns(g, depth) for g in by_columns]
+    piece_rows = pieces[0].shape[5]
+    by_rows = [bf16[6], bf16[3]]
+    pieces = pieces[:2] + [split_rows(by_rows[0], depth, piece_rows)] + pieces[2:]
+    pieces = pieces + [split_rows(by_rows[1], depth, piece_rows)]
+    gain_terms = attn_gradients[4:6] + ff_gradients[3:5] + attn_gradients[6:8]
+    gain_rows = jnp.concatenate(gain_terms).astype(jnp.bfloat16).astype(jnp.float32)
+    summed, gain_sums = reduce_terms(
+        jnp.concatenate(pieces, axis=0), gain_rows.reshape(-1, LANES)
+    )
+    bounds = [0]
+    for piece in pieces:
+        bounds.append(bounds[-1] + piece.shape[0])
+    cuts = [summed[low:high].astype(jnp.float32) for low, high in zip(bounds[:-1], bounds[1:])]
+    sum_gate, sum_up, sum_query, sum_key_value = [
+        join_columns(cuts[i]) for i in (0, 1, 3, 4)
+    ]
+    sum_down = join_rows(cuts[2], by_rows[0].shape[1])
+    sum_out = join_rows(cuts[5], by_rows[1].shape[1])
+    me = lax.axis_index("wshard")
+    gain_sums = gain_sums[3].reshape(-1)
+    gain_outs = []
+    start = 0
+    for term in gain_terms:
+        half = term.shape[0] // 2
+        gain_outs.append(lax.dynamic_slice_in_dim(gain_sums, start + me * half, half))
+        start += term.shape[0]
+    return (
+        layer_out, grad_inputs, sum_query, sum_key_value[:, :head_dim], sum_key_value[:, head_dim:],
+        sum_out, sum_gate, sum_up, sum_down,
+    ) + tuple(gain_outs)
+
+
+def per_device_general(
     inputs,
     doc_ids,
     w_query,
@@ -346,8 +889,9 @@
 
 
 def solution(mesh):
+    routed = mesh.shape["wshard"] == 2 and mesh.shape["seq"] == 16
     return jax.shard_map(
-        per_device,
+        per_device if routed else per_device_general,
         mesh=mesh,
         in_specs=(
             P(("seq", "wshard"), None),

time: 602 us -> 372 us (0.62)
  waiting for transfers between devices: 382 us -> 0.03 us
  Pallas kernels: 0 us -> 152 us
  local copies, waits for them, and re-layouts: 15.4 us -> 104 us
  blocking collectives: 72.1 us -> 0 us
  between operations: 17 us -> 1.63 us
  matrix products: 61.4 us -> 53.6 us
    reduce_scatter x7 -> x0, waiting for transfers between devices: 185 us -> none  [the longest x1 40.5 us: per_device(): lax.psum_scatter(ff_gradients[1].astype(jnp.bfloat16), 'wshard', scatter_...]
    pallas_call x0 -> x2, Pallas kernels: none -> 152 us  [the longest x1 104 us: reduce_terms(): pl.pallas_call(reduce_kernel, out_shape=[jax.ShapeDtypeStruct((chunks, 2,...]
    all_gather x5 -> x0, waiting for transfers between devices: 105 us -> none  [the longest x1 36.4 us: per_device(): lax.all_gather(w_up, 'wshard', axis=0, tiled=True)]
    psum x1 -> x0, waiting for transfers between devices: 87.6 us -> none  [per_device(): lax.psum(attn_parts[0].astype(jnp.bfloat16), 'seq').astype(jnp.float32)]
    reshape x0 -> x16, local copies, waits for them, and re-layouts: none -> 53.7 us  [the longest x5 22.4 us: split_columns(): term.reshape(2, 2, 2, rows // 8, columns // (depth * LANES), depth, LANES)]
    psum x1 -> x0, blocking collectives: 34.5 us -> none  [per_device(): lax.psum(attn_parts[4].astype(jnp.bfloat16), 'seq').astype(jnp.float32)]
    all_gather x4 -> x0, blocking collectives: 26.6 us -> none  [the longest x1 9.77 us: per_device(): lax.all_gather(w_value, 'wshard', axis=0, tiled=True)]
    convert_element_type x13 -> x2, other arithmetic: 15.5 us -> 0.01 us  [the longest x1 0.01 us: per_device(): jnp.concatenate(small).astype(jnp.float32).reshape(1, -1, LANES)]
  transfers between devices with their start and end apart: 23 -> 10, of which waited for: 11 -> 0; matrix products, arithmetic and copies ran while one was open for 10% -> 24% of each run, Pallas kernels for 0% -> 0%
where the time goes in v1:
time: 372 us; the launch traced here: 366 us
  Pallas kernels  152 us (41%)
  local copies, waits for them, and re-layouts  104 us (28%)
  matrix products  53.6 us (14%)
  other arithmetic  31.8 us (9%)
  starting transfers between devices  22.2 us (6%)
    pallas_call x1, Pallas kernels, reduce_terms(): pl.pallas_call(reduce_kernel, out_shape=[jax.ShapeDtypeStruct((chunks, 2,...  104 us
    pallas_call x1, Pallas kernels, gather_weights(): pl.pallas_call(functools.partial(gather_kernel, count), out_shape=[jax.Sh...  48.6 us
    unnamed x126, local copies, waits for them, and re-layouts  26 us
    reshape x5, local copies, waits for them, and re-layouts, split_columns(): term.reshape(2, 2, 2, rows // 8, columns // (depth * LANES), depth, LANES)  22.4 us
    ppermute x10, starting transfers between devices, from_behind(): return lax.ppermute(array, axis, pairs)  22.2 us
    reshape x7, local copies, waits for them, and re-layouts, join_columns(): pieces.transpose(1, 2, 4, 0, 3, 5).reshape(4 * rows, chunks * depth * lanes)  19.6 us
    dot_general x7, matrix products, weight_grad(): jnp.einsum('tc,tf->cf', left_rows, right_rows, preferred_element_type=jnp...  11.3 us
    reshape x2, local copies, waits for them, and re-layouts, split_rows(): term = term.reshape(2, chunks, 2, 2, depth, high, tiles, LANES)  11.1 us
  transfers between devices with their start and end apart: 10, of which 0 were waited for; matrix products, arithmetic and copies ran while one was open for 24% of the time, Pallas kernels for 0%

profile of v1, /device:TPU:0, one launch (start us, length us, event | category | flops | bytes accessed | tf_op | source)
XLA Modules:
  0.0 365.9 jit_solution(6277405309076711447)
XLA Ops:
  0.6 4.2 %concatenate.30 = bf16[1536]{0:T(1024)(128)(2,1)S(1)} concatenate(bf16[320]{0:T(512)(128)(2,1)} %param.25, bf16[320]{0:T(512)(128)(2,1)} %param.26, bf16[320]{0:T(512)(128)(2,1)} %param.27, bf16[320]{0:T(512)(128)(2,1)} %param.28, bf16[128]{0:T(256)(128)(2,1)} %param.29, bf16[128]{0:T(256)(128)(2,1)} %param.30), dimensions={0} | concatenate | bytes 6144 | tf_op jit(solution)/shard_map/concatenate | solution.py:410
  8.8 48.6 %gather_weights.1 = (bf16[640,1024]{1,0:T(8,128)(2,1)S(1)}, bf16[640,256]{1,0:T(8,128)(2,1)S(1)}, bf16[640,256]{1,0:T(8,128)(2,1)S(1)}, bf16[1024,640]{1,0:T(8,1...) custom-call(bf16[320,1024]{1,0:T(8,128)(2,1)S(1)} %copy-done, ...), custom_call_target="tpu_custom_call" | custom-call | tf_op jit(solution)/shard_map/gather_weights/pallas_call | solution.py:168
  61.3 3.2 collective-permute-start.1
  66.6 3.9 %collective-permute-start.3 = (s32[256]{0:T(256)}, s32[256]{0:T(256)}, u32[]{:S(2)}, u32[]{:S(2)}) collective-permute-start(s32[256]{0:T(256)} %param.17), channel_id=1, source_target_pairs={{0,1},{1,2},{2,3},{3,4},{4,5},{5,6},{6,7},{7,8},{8,9},{9,10},{10,1... | collective-permute-start | bytes 3080 | tf_op jit(solution)/shard_map/ppermute | solution.py:21
  76.9 2.6 collective-permute-start.5
  83.9 2.6 fusion.85
  86.5 2.7 reshape.511
  98.5 3.3 collective-permute-start.4
  117.4 2.6 multiply_convert_fusion
  121.0 2.4 convolution_convert_fusion.2
  123.4 2.5 convolution_convert_fusion
  133.8 3.4 fusion.39
  137.2 8.1 %fusion.97 = (bf16[768,256]{0,1:T(8,128)(2,1)S(1)}, f32[768,256]{0,1:T(8,128)}) fusion(bf16[256,4,128]{2,0,1:T(8,128)(2,1)S(1)} %copy-done.28, bf16[256,4,128]{2,0,1:T(8,128)(2,1)S(1)} %copy-done.27, f32[768,256,4]{1,0,2:T(8,128)} %fusion.39, f32[4,256]{1,0:T(4,128)S(1)} %copy-done.50, f32[768,256,4]{1,0,2:T(8,128)} %copy-done.14, ...), kind=kOutput, calls=%fused_computation.207 | convolution fusion | flops 414123776 | bytes 8196096 | tf_op jit(solution)/shard_map/hqk,qhd->kd/dot_general | solution.py:513
  148.7 6.7 %fusion.15 = f32[256,4,256]{2,0,1:T(8,128)S(1)} fusion(f32[768,256,4]{1,0,2:T(8,128)} %fusion.39, bf16[256,256]{0,1:T(8,128)(2,1)} %maximum_bitcast_fusion.6, bf16[256,256]{0,1:T(8,128)(2,1)} %collective-permute-done.5, bf16[256,256]{0,1:T(8,128)(2,1)} %copy-done.55, f32[768,256,4]{1,0,2:T(8,128)} %copy-done.14, f32[4,256]{1,0:T(4,128)S(1)} %copy-done.50, ...), kind=kOutput, calls=%fused_computation.36 | convolution fusion | flops 414058240 | bytes 7933952 | tf_op jit(solution)/shard_map/hqk,kd->qhd/dot_general | solution.py:510
  163.2 5.4 %reshape.513 = bf16[2,2,2,80,4,4,128]{6,5,4,3,2,1,0:T(4,128)(2,1)} reshape(bf16[640,2048]{1,0:T(8,128)(2,1)} %convolution_convert_fusion.2) | data formatting | bytes 5242880 | tf_op jit(solution)/shard_map/reshape | solution.py:364
  168.6 3.9 %bitcast_dynamic-update-slice_fusion.1 = bf16[17,2,2,2,4,80,128]{6,5,4,3,2,1,0:T(8,128)(2,1)} fusion(bf16[2,2,2,80,4,4,128]{6,5,4,3,2,1,0:T(4,128)(2,1)} %reshape.513), kind=kLoop, calls=%fused_computation.16 | loop fusion | bytes 5242880
  172.6 5.4 %reshape.514 = bf16[2,2,2,80,4,4,128]{6,5,4,3,2,1,0:T(4,128)(2,1)} reshape(bf16[640,2048]{1,0:T(8,128)(2,1)} %convolution_convert_fusion.1) | data formatting | bytes 5242880 | tf_op jit(solution)/shard_map/reshape | solution.py:364
  178.0 7.0 %reshape.515 = bf16[2,4,2,2,4,16,5,128]{7,6,5,4,3,2,1,0:T(8,128)(2,1)} reshape(bf16[2048,640]{1,0:T(8,128)(2,1)} %convolution_convert_fusion) | data formatting | bytes 5242880 | tf_op jit(solution)/shard_map/reshape | solution.py:378
  185.0 4.5 %copy.147 = bf16[4,2,2,2,4,5,16,128]{7,6,5,4,3,2,1,0:T(8,128)(2,1)} copy(bf16[4,2,2,2,4,5,16,128]{7,5,6,4,3,1,0,2:T(8,128)(2,1)} %bitcast.234) | data formatting | bytes 5242880 | tf_op jit(solution)/shard_map/transpose | solution.py:379
  191.2 3.8 %reshape.517 = bf16[2,2,2,80,2,4,128]{6,5,4,3,2,1,0:T(4,128)(2,1)} reshape(bf16[640,1024]{1,0:T(8,128)(2,1)} %convolution_convert_fusion.4) | data formatting | bytes 2621440 | tf_op jit(solution)/shard_map/reshape | solution.py:364
  195.0 4.1 %bitcast_dynamic-update-slice_fusion = bf16[17,2,2,2,4,80,128]{6,5,4,3,2,1,0:T(8,128)(2,1)} fusion(bf16[17,2,2,2,4,80,128]{6,5,4,3,2,1,0:T(8,128)(2,1)} %bitcast_dynamic-update-slice_fusion.1, bf16[2,2,2,80,4,4,128]{6,5,4,3,2,1,0:T(4,128)(2,1)} %reshape.514), kind=kLoop, calls=%fused_computation.15 | loop fusion | bytes 5242880
  203.9 4.1 %reshape.519 = bf16[2,2,2,2,4,16,5,128]{7,6,5,4,3,2,1,0:T(8,128)(2,1)} reshape(bf16[1024,640]{1,0:T(8,128)(2,1)} %convolution_convert_fusion.3) | data formatting | bytes 2621440 | tf_op jit(solution)/shard_map/reshape | solution.py:378
  208.0 3.0 copy.151
  218.0 5.4 %reshape.565 = bf16[2,2,2,80,1,4,128]{3,2,1,0,6,5,4:T(2,128)(2,1)S(1)} reshape(bf16[640,512]{0,1:T(8,128)(2,1)} %pad_maximum_fusion) | data formatting | bytes 1310720 | tf_op jit(solution)/shard_map/reshape | solution.py:364
  223.4 2.4 copy.150
  230.1 103.7 %reduce_terms.1 = (bf16[17,2,2,4,80,128]{5,4,3,2,1,0:T(8,128)(2,1)S(1)}, f32[4,24,128]{2,1,0:T(8,128)S(1)}) custom-call(bf16[17,2,2,2,4,80,128]{6,5,4,3,2,1,0:T(8,128)(2,1)} %constant_dynamic-update-slice_fusion.terms, f32[24,128]{1,0:T(8,128)S(1)} %bitcast_convert_fusion.gains), custom_call_target="tpu_custom_call" | custom-call | tf_op jit(solution)/shard_map/reduce_terms/pallas_call | solution.py:338
  334.9 3.1 fusion.90
  339.6 2.7 reshape.538
  345.7 2.5 copy.155
  348.2 4.1 %reshape.544 = f32[320,2048]{1,0:T(8,128)} reshape(f32[2,2,80,4,4,128]{5,4,3,2,1,0:T(4,128)} %copy.155) | data formatting | bytes 5242880 | tf_op jit(solution)/shard_map/reshape | solution.py:370
  352.3 4.3 %copy.156 = f32[2,2,80,4,4,128]{5,4,3,2,1,0:T(4,128)} copy(f32[2,2,80,4,4,128]{5,2,4,1,0,3:T(8,128)} %get-tuple-element.51) | data formatting | bytes 5242880 | tf_op jit(solution)/shard_map/reshape | solution.py:370
  356.6 4.2 %reshape.546 = f32[320,2048]{1,0:T(8,128)} reshape(f32[2,2,80,4,4,128]{5,4,3,2,1,0:T(4,128)} %copy.156) | data formatting | bytes 5242880 | tf_op jit(solution)/shard_map/reshape | solution.py:370
  (230 shorter events, 93.9 us)
Async XLA Ops:
  59.3 15.5 %copy-start.42 = (f32[256]{0:T(256)}, f32[256]{0:T(256)S(1)}, u32[]{:S(2)}) copy-start(f32[256]{0:T(256)S(1)} %fusion.36) | copy-start | bytes 3076
  59.4 27.2 %copy-start.33 = (f32[256]{0:T(256)}, f32[256]{0:T(256)S(1)}, u32[]{:S(2)}) copy-start(f32[256]{0:T(256)S(1)} %fusion.67) | copy-start | bytes 3076
  61.3 45.6 %collective-permute-start.1 = (bf16[256,256]{1,0:T(8,128)(2,1)}, bf16[256,256]{1,0:T(8,128)(2,1)}, u32[]{:S(2)}, u32[]{:S(2)}) collective-permute-start(bf16[256,256]{1,0:T(8,128)(2,1)} %convolution_convert_fusion.9), channel_id=1, source_target_pairs={{0,1},{1,2},{2,3},{3,4},{4,5},{5,6},{6,7},{7,8},{8,9},{9,10},{10,1... | collective-permute-start | bytes 393224 | tf_op jit(solution)/shard_map/ppermute | solution.py:21
  64.5 42.4 %collective-permute-start = (bf16[256,256]{1,0:T(8,128)(2,1)}, bf16[256,256]{1,0:T(8,128)(2,1)}, u32[]{:S(2)}, u32[]{:S(2)}) collective-permute-start(bf16[256,256]{1,0:T(8,128)(2,1)} %convolution_convert_fusion.9), channel_id=1, source_target_pairs={{0,2},{1,3},{2,4},{3,5},{4,6},{5,7},{6,8},{7,9},{8,10},{9,11},{10,... | collective-permute-start | bytes 393224 | tf_op jit(solution)/shard_map/ppermute | solution.py:21
  66.6 31.9 %collective-permute-start.3 = (s32[256]{0:T(256)}, s32[256]{0:T(256)}, u32[]{:S(2)}, u32[]{:S(2)}) collective-permute-start(s32[256]{0:T(256)} %param.17), channel_id=1, source_target_pairs={{0,1},{1,2},{2,3},{3,4},{4,5},{5,6},{6,7},{7,8},{8,9},{9,10},{10,1... | collective-permute-start | bytes 3080 | tf_op jit(solution)/shard_map/ppermute | solution.py:21
  70.5 31.2 %collective-permute-start.2 = (s32[256]{0:T(256)}, s32[256]{0:T(256)}, u32[]{:S(2)}, u32[]{:S(2)}) collective-permute-start(s32[256]{0:T(256)} %param.17), channel_id=1, source_target_pairs={{0,2},{1,3},{2,4},{3,5},{4,6},{5,7},{6,8},{7,9},{8,10},{9,11},{10,... | collective-permute-start | bytes 3080 | tf_op jit(solution)/shard_map/ppermute | solution.py:21
  72.9 16.3 %copy-start.37 = (f32[256]{0:T(256)}, f32[256]{0:T(256)S(1)}, u32[]{:S(2)}) copy-start(f32[256]{0:T(256)S(1)} %get-tuple-element.83) | copy-start | bytes 3076
  74.9 4.7 %copy-start.51 = (f32[256]{0:T(256)}, f32[256]{0:T(256)S(1)}, u32[]{:S(2)}) copy-start(f32[256]{0:T(256)S(1)} %get-tuple-element.87) | copy-start | bytes 3076
  74.9 8.3 %copy-start.35 = (f32[256]{0:T(256)}, f32[256]{0:T(256)S(1)}, u32[]{:S(2)}) copy-start(f32[256]{0:T(256)S(1)} %fusion.68) | copy-start | bytes 3076
  76.9 27.2 %collective-permute-start.5 = (bf16[256,256]{0,1:T(8,128)(2,1)}, bf16[256,256]{0,1:T(8,128)(2,1)}, u32[]{:S(2)}, u32[]{:S(2)}) collective-permute-start(bf16[256,256]{0,1:T(8,128)(2,1)} %maximum_bitcast_fusion.6), channel_id=1, source_target_pairs={{0,1},{1,2},{2,3},{3,4},{4,5},{5,6},{6,7},{7,8},{8,9},{9,10},{10,1... | collective-permute-start | bytes 393224 | tf_op jit(solution)/shard_map/ppermute | solution.py:21
  98.5 5.7 %collective-permute-start.4 = (bf16[256,256]{0,1:T(8,128)(2,1)}, bf16[256,256]{0,1:T(8,128)(2,1)S(1)}, u32[]{:S(2)}, u32[]{:S(2)}) collective-permute-start(bf16[256,256]{0,1:T(8,128)(2,1)} %maximum_bitcast_fusion.6), channel_id=1, source_target_pairs={{0,2},{1,3},{2,4},{3,5},{4,6},{5,7},{6,8},{7,9},{8,10},{9,11},{10,... | collective-permute-start | bytes 393224 | tf_op jit(solution)/shard_map/ppermute | solution.py:21
  104.1 27.6 %copy-start.26 = (pred[256,768]{0,1:T(8,128)(4,1)}, pred[256,768]{0,1:T(8,128)(4,1)S(1)}, u32[]{:S(2)}) copy-start(pred[256,768]{0,1:T(8,128)(4,1)S(1)} %fusion.24) | copy-start | bytes 589828
  106.2 25.6 %copy-start.14 = (f32[768,256,4]{1,0,2:T(8,128)}, f32[768,256,4]{1,0,2:T(8,128)S(1)}, u32[]{:S(2)}) copy-start(f32[768,256,4]{1,0,2:T(8,128)S(1)} %get-tuple-element.90) | copy-start | bytes 9437188
  107.0 24.8 %copy-start.49 = (f32[4,256]{1,0:T(4,128)}, f32[4,256]{1,0:T(4,128)S(1)}, u32[]{:S(2)}) copy-start(f32[4,256]{1,0:T(4,128)S(1)} %log_add_fusion) | copy-start | bytes 12292
  145.9 65.1 %collective-permute-start.7 = (bf16[256,256]{0,1:T(8,128)(2,1)}, bf16[256,256]{0,1:T(8,128)(2,1)}, u32[]{:S(2)}, u32[]{:S(2)}) collective-permute-start(bf16[256,256]{0,1:T(8,128)(2,1)} %get-tuple-element.68), channel_id=1, source_target_pairs={{1,0},{2,1},{3,2},{4,3},{5,4},{6,5},{7,6},{8,7},{9,8},{10,9},{11,1... | collective-permute-start | bytes 393224 | tf_op jit(solution)/shard_map/ppermute | solution.py:21
  147.2 8.2 %copy-start.24 = (f32[256,128]{1,0:T(8,128)S(1)}, f32[256,128]{1,0:T(8,128)}, u32[]{:S(2)}) copy-start(f32[256,128]{1,0:T(8,128)} %get-tuple-element.85) | copy-start | bytes 393220
  147.2 8.2 %copy-start.25 = (f32[256,128]{1,0:T(8,128)S(1)}, f32[256,128]{1,0:T(8,128)}, u32[]{:S(2)}) copy-start(f32[256,128]{1,0:T(8,128)} %get-tuple-element.86) | copy-start | bytes 393220
  147.3 8.3 %copy-start.39 = (f32[256]{0:T(256)S(1)}, f32[256]{0:T(256)}, u32[]{:S(2)}) copy-start(f32[256]{0:T(256)} %get-tuple-element.84) | copy-start | bytes 3076
  147.3 63.7 %collective-permute-start.6 = (bf16[256,256]{0,1:T(8,128)(2,1)}, bf16[256,256]{0,1:T(8,128)(2,1)}, u32[]{:S(2)}, u32[]{:S(2)}) collective-permute-start(bf16[256,256]{0,1:T(8,128)(2,1)} %get-tuple-element.67), channel_id=1, source_target_pairs={{2,0},{3,1},{4,2},{5,3},{6,4},{7,5},{8,6},{9,7},{10,8},{11,9},{12,... | collective-permute-start | bytes 393224 | tf_op jit(solution)/shard_map/ppermute | solution.py:21
  160.6 53.7 %collective-permute-start.9 = (bf16[256,256]{1,0:T(8,128)(2,1)}, bf16[256,256]{1,0:T(8,128)(2,1)}, u32[]{:S(2)}, u32[]{:S(2)}) collective-permute-start(bf16[256,256]{1,0:T(8,128)(2,1)} %get-tuple-element.66), channel_id=1, source_target_pairs={{1,0},{2,1},{3,2},{4,3},{5,4},{6,5},{7,6},{8,7},{9,8},{10,9},{11,1... | collective-permute-start | bytes 393224 | tf_op jit(solution)/shard_map/ppermute | solution.py:21
  161.9 52.4 %collective-permute-start.8 = (bf16[256,256]{1,0:T(8,128)(2,1)}, bf16[256,256]{1,0:T(8,128)(2,1)}, u32[]{:S(2)}, u32[]{:S(2)}) collective-permute-start(bf16[256,256]{1,0:T(8,128)(2,1)} %get-tuple-element.65), channel_id=1, source_target_pairs={{2,0},{3,1},{4,2},{5,3},{6,4},{7,5},{8,6},{9,7},{10,8},{11,9},{12,... | collective-permute-start | bytes 393224 | tf_op jit(solution)/shard_map/ppermute | solution.py:21
  185.0 4.6 %copy-start.6 = (bf16[256,640]{1,0:T(8,128)(2,1)S(1)}, bf16[256,640]{1,0:T(8,128)(2,1)}, u32[]{:S(2)}) copy-start(bf16[256,640]{1,0:T(8,128)(2,1)} %param.16) | copy-start | bytes 983044
  185.0 4.6 %copy-start.34 = (f32[256]{0:T(256)S(1)}, f32[256]{0:T(256)}, u32[]{:S(2)}) copy-start(f32[256]{0:T(256)} %copy-done.33) | copy-start | bytes 3076
  208.0 4.7 %copy-start.36 = (f32[256]{0:T(256)S(1)}, f32[256]{0:T(256)}, u32[]{:S(2)}) copy-start(f32[256]{0:T(256)} %copy-done.35) | copy-start | bytes 3076
  208.0 4.7 %copy-start.38 = (f32[256]{0:T(256)S(1)}, f32[256]{0:T(256)}, u32[]{:S(2)}) copy-start(f32[256]{0:T(256)} %copy-done.37) | copy-start | bytes 3076
  208.0 4.9 %copy-start.52 = (f32[256]{0:T(256)S(1)}, f32[256]{0:T(256)}, u32[]{:S(2)}) copy-start(f32[256]{0:T(256)} %copy-done.51) | copy-start | bytes 3076
  217.0 8.7 %copy-start.47 = (bf16[3072]{0:T(1024)(128)(2,1)S(1)}, bf16[3072]{0:T(1024)(128)(2,1)}, u32[]{:S(2)}) copy-start(bf16[3072]{0:T(1024)(128)(2,1)} %custom-call) | copy-start | bytes 18436
  217.0 8.9 %copy-start.46 = (bf16[640]{0:T(1024)(128)(2,1)S(1)}, bf16[640]{0:T(1024)(128)(2,1)}, u32[]{:S(2)}) copy-start(bf16[640]{0:T(1024)(128)(2,1)} %get-tuple-element.39) | copy-start | bytes 3844
  217.0 9.1 %copy-start.45 = (bf16[640]{0:T(1024)(128)(2,1)S(1)}, bf16[640]{0:T(1024)(128)(2,1)}, u32[]{:S(2)}) copy-start(bf16[640]{0:T(1024)(128)(2,1)} %get-tuple-element.37) | copy-start | bytes 3844
  217.0 9.3 %copy-start.44 = (bf16[640]{0:T(1024)(128)(2,1)S(1)}, bf16[640]{0:T(1024)(128)(2,1)}, u32[]{:S(2)}) copy-start(bf16[640]{0:T(1024)(128)(2,1)} %get-tuple-element.41) | copy-start | bytes 3844
  217.0 9.5 %copy-start.53 = (bf16[256]{0:T(256)(128)(2,1)S(1)}, bf16[256]{0:T(256)(128)(2,1)}, u32[]{:S(2)}) copy-start(bf16[256]{0:T(256)(128)(2,1)} %get-tuple-element.35) | copy-start | bytes 1540
  218.0 11.0 %copy-start.11 = (bf16[2,2,2,2,4,5,16,128]{7,6,5,4,3,2,1,0:T(8,128)(2,1)S(1)}, bf16[2,2,2,2,4,5,16,128]{7,6,5,4,3,2,1,0:T(8,128)(2,1)}, u32[]{:S(2)}) copy-start(bf16[2,2,2,2,4,5,16,128]{7,6,5,4,3,2,1,0:T(8,128)(2,1)} %copy.151) | copy-start | bytes 3932164
  (34 other events, 73.6 us)

commit v2 on v1

--- a/solution.py
+++ b/solution.py
@@ -182,9 +182,35 @@
     )(*shards)
 
 
+def term_groups(lefts, rights, depth):
+    groups = []
+    for left, right in zip(lefts, rights):
+        columns = right.shape[1]
+        by_columns = columns % (depth * LANES) == 0
+        piece = lefts[0].shape[1] // 8 * LANES
+        if by_columns:
+            chunks = columns // (depth * LANES)
+        else:
+            chunks = left.shape[1] * columns // (8 * depth * piece)
+        groups.append((left, right, by_columns, chunks))
+    return groups
+
+
 def reduce_kernel(
-    terms, gains, out, gains_out,
-    from_core, from_across, from_beside, from_line, gain_in,
+    count, *refs
+):
+    reduce_body(refs[:count], refs[count : 2 * count], *refs[2 * count :])
+
+
+def token_dot(left, right):
+    return lax.dot_general(
+        left, right, (((0,), (0,)), ((), ())), preferred_element_type=jnp.float32
+    ).astype(jnp.bfloat16)
+
+
+def reduce_body(
+    lefts, rights, gains, out, gains_out,
+    terms, from_core, from_across, from_beside, from_line, gain_in,
     send_core, recv_core, send_across, recv_across, send_beside, recv_beside,
     send_line, recv_line, send_zline, recv_zline, send_xback, recv_xback,
     send_back, recv_back, send_gain, recv_gain,
@@ -241,11 +267,47 @@
     def add(a, b):
         return (a.astype(jnp.float32) + b.astype(jnp.float32)).astype(jnp.bfloat16)
 
-    @pl.loop(0, chunks)
-    def _(c):
-        to_core(c).start()
-
     gain_copy(0).start()
+    piece_rows = terms.shape[5]
+
+    def make_columns(left, right, at, c):
+        width = depth * LANES
+        block = token_dot(left[...], right[:, pl.ds(pl.multiple_of(at * width, width), width)])
+        for side in range(2):
+            for own in range(2):
+                for across_x in range(2):
+                    low = ((side * 2 + own) * 2 + across_x) * piece_rows
+                    for place in range(depth):
+                        terms[c, own, side, across_x, place] = block[
+                            low : low + piece_rows, place * LANES : (place + 1) * LANES
+                        ]
+
+    def make_rows(left, right, at, c, parts):
+        rows, tiles = left.shape[1] // (2 * parts), right.shape[1] // LANES
+        high = rows // (4 * depth)
+        for side in range(2):
+            start = pl.multiple_of((side * parts + at) * rows, rows)
+            block = token_dot(left[:, pl.ds(start, rows)], right[...])
+            for own in range(2):
+                for across_x in range(2):
+                    for place in range(depth):
+                        low = ((own * 2 + across_x) * depth + place) * high
+                        for tile in range(tiles):
+                            terms[
+                                c, own, side, across_x, place, tile * high : (tile + 1) * high
+                            ] = block[low : low + high, tile * LANES : (tile + 1) * LANES]
+
+    def make(t):
+        start = 0
+        for left, right, by_columns, parts in term_groups(lefts, rights, depth):
+            @pl.when((t >= start) & (t < start + parts))
+            def _(left=left, right=right, by_columns=by_columns, parts=parts, start=start):
+                if by_columns:
+                    make_columns(left, right, t - start, t)
+                else:
+                    make_rows(left, right, t - start, t, parts)
+            start += parts
+        to_core(t).start()
 
     def stage(at, action):
         @pl.when((at >= 0) & (at < chunks))
@@ -288,7 +350,7 @@
         back_beside(c, 1 - x).wait_recv()
         back_core(c, core).start()
 
-    actions = [after_core, after_across, after_beside, after_line, after_zline, after_xback]
+    actions = [make, after_core, after_across, after_beside, after_line, after_zline, after_xback]
 
     @pl.loop(0, chunks + len(actions) - 1)
     def _(t):
@@ -327,23 +389,26 @@
         back_core(c, core).wait_send()
 
 
-def reduce_terms(terms, gains):
-    chunks, _, _, _, depth, rows, lanes = terms.shape
-    piece = (rows, lanes)
+def reduce_terms(lefts, rights, gains):
+    depth = lax.axis_size("seq") // 4
+    groups = term_groups(lefts, rights, depth)
+    chunks = sum(group[3] for group in groups)
+    piece = (lefts[0].shape[1] // 8, LANES)
     dma = pltpu.SemaphoreType.DMA
     vmem = pl.BlockSpec(memory_space=pltpu.VMEM)
     pair = [dma((chunks,)), dma((chunks,))]
     lines = [dma((chunks, depth - 1)), dma((chunks, depth - 1))]
     steps = 2 + depth
     return pl.pallas_call(
-        reduce_kernel,
+        functools.partial(reduce_kernel, len(lefts)),
         out_shape=[
             jax.ShapeDtypeStruct((chunks, 2, 2, depth) + piece, jnp.bfloat16),
             jax.ShapeDtypeStruct((4,) + gains.shape, jnp.float32),
         ],
-        in_specs=[vmem, vmem],
+        in_specs=[vmem] * (2 * len(lefts) + 1),
         out_specs=[vmem, vmem],
         scratch_shapes=[
+            pltpu.VMEM((chunks, 2, 2, 2, depth) + piece, jnp.bfloat16),
             pltpu.VMEM((chunks, 2, 2, depth) + piece, jnp.bfloat16),
             pltpu.VMEM((chunks, 2, depth) + piece, jnp.bfloat16),
             pltpu.VMEM((chunks, depth) + piece, jnp.bfloat16),
@@ -353,39 +418,72 @@
         + pair + pair + pair + lines + lines + pair + pair
         + [dma((steps,)), dma((steps,))],
         compiler_params=pltpu.CompilerParams(
-            collective_id=2, has_side_effects=True, vmem_limit_bytes=48 * 2**20
+            collective_id=2, has_side_effects=True, vmem_limit_bytes=56 * 2**20
         ),
         name="reduce_terms",
-    )(terms, gains)
-
-
-def split_columns(term, depth):
-    rows, columns = term.shape
-    term = term.reshape(2, 2, 2, rows // 8, columns // (depth * LANES), depth, LANES)
-    return term.transpose(4, 1, 0, 2, 5, 3, 6)
-
-
-def join_columns(pieces):
-    chunks, _, _, depth, rows, lanes = pieces.shape
-    return pieces.transpose(1, 2, 4, 0, 3, 5).reshape(4 * rows, chunks * depth * lanes)
-
-
-def split_rows(term, depth, piece_rows):
-    rows, columns = term.shape
-    tiles = columns // LANES
-    high = piece_rows // tiles
-    chunks = rows // (8 * depth * high)
-    term = term.reshape(2, chunks, 2, 2, depth, high, tiles, LANES)
-    term = term.transpose(1, 2, 0, 3, 4, 6, 5, 7)
-    return term.reshape(chunks, 2, 2, 2, depth, tiles * high, LANES)
-
-
-def join_rows(pieces, columns):
-    chunks, _, _, depth, piece_rows, lanes = pieces.shape
-    tiles = columns // lanes
-    high = piece_rows // tiles
-    pieces = pieces.reshape(chunks, 2, 2, depth, tiles, high, lanes).transpose(0, 1, 2, 3, 5, 4, 6)
-    return pieces.reshape(chunks * 4 * depth * high, columns)
+    )(*lefts, *rights, gains)
+
+
+def unpack_kernel(plan, summed, *outs):
+    c = pl.program_id(0)
+    depth, rows = summed.shape[3], summed.shape[4]
+    for outputs, by_columns, start, parts in plan:
+        @pl.when((c >= start) & (c < start + parts))
+        def _(outputs=outputs, by_columns=by_columns):
+            for core in range(2):
+                for x in range(2):
+                    for z in range(depth):
+                        piece = summed[0, core, x, z].astype(jnp.float32)
+                        if by_columns:
+                            low = (core * 2 + x) * rows
+                            ref, column = outputs[0], z * LANES
+                            width = outs[ref].shape[1]
+                            ref, column = ref + column // width, column % width
+                            outs[ref][low : low + rows, column : column + LANES] = piece
+                        else:
+                            ref = outs[outputs[0]]
+                            tiles = ref.shape[1] // LANES
+                            high = rows // tiles
+                            low = ((core * 2 + x) * depth + z) * high
+                            for tile in range(tiles):
+                                ref[low : low + high, tile * LANES : (tile + 1) * LANES] = piece[
+                                    tile * high : (tile + 1) * high
+                                ]
+
+
+def unpack(summed, shapes):
+    chunks, _, _, depth, rows, lanes = summed.shape
+    width = depth * lanes
+    plan, shaped, specs, start, index = [], [], [], 0, 0
+    while index < len(shapes):
+        high, wide = shapes[index]
+        together = max(1, width // wide) if wide <= width and width % wide == 0 else 1
+        by_columns = (wide * together) % width == 0
+        if by_columns:
+            parts = wide * together // width
+            block = (high, min(wide, width))
+        else:
+            parts = high * wide // (4 * depth * rows * lanes)
+            block = (high // parts, wide)
+        plan.append((list(range(index, index + together)), by_columns, start, parts))
+
+        def place(c, start=start, parts=parts, by_columns=by_columns):
+            at = jnp.clip(c - start, 0, parts - 1)
+            return (0, at) if by_columns else (at, 0)
+
+        for k in range(together):
+            shaped.append(jax.ShapeDtypeStruct(shapes[index + k], jnp.float32))
+            specs.append(pl.BlockSpec(block, place))
+        start += parts
+        index += together
+    return pl.pallas_call(
+        functools.partial(unpack_kernel, plan),
+        grid=(chunks,),
+        out_shape=shaped,
+        in_specs=[pl.BlockSpec((1,) + summed.shape[1:], lambda c: (c, 0, 0, 0, 0, 0))],
+        out_specs=specs,
+        name="unpack",
+    )(summed)
 
 
 def per_device(
@@ -472,7 +570,6 @@
     _, pullback = jax.vjp(rms_gain, ff_proj, ff_post_gain)
     grad_ff_proj, grad_gain_ff_post = pullback(grad_top)
     grad_ff_proj = grad_ff_proj.astype(jnp.bfloat16)
-    grad_w_down = weight_grad(hidden, grad_ff_proj)
     grad_hidden = lax.dot_general(
         grad_ff_proj, full_down, (((1,), (1,)), ((), ())), preferred_element_type=jnp.float32
     )
@@ -480,8 +577,6 @@
     grad_gate, grad_up = pullback(grad_hidden)
     grad_gate = grad_gate.astype(jnp.bfloat16)
     grad_up = grad_up.astype(jnp.bfloat16)
-    grad_w_gate = weight_grad(normed_ff, grad_gate)
-    grad_w_up = weight_grad(normed_ff, grad_up)
     grad_normed_ff = lax.dot_general(
         grad_gate, full_gate, (((1,), (1,)), ((), ())), preferred_element_type=jnp.float32
     )
@@ -491,11 +586,9 @@
     _, pullback = jax.vjp(rms_gain, resid, ff_pre_gain)
     grad_resid_part, grad_gain_ff_pre = pullback(grad_normed_ff)
     grad_resid = grad_top + grad_resid_part
-    ff_gradients = (grad_w_gate, grad_w_up, grad_w_down, grad_gain_ff_pre, grad_gain_ff_post)
     _, pullback = jax.vjp(rms_gain, attn_proj, attn_post_gain)
     grad_attn_proj, grad_gain_attn_post = pullback(grad_resid)
     grad_attn_proj = grad_attn_proj.astype(jnp.bfloat16)
-    grad_w_out = weight_grad(attended, grad_attn_proj)
     grad_attended = lax.dot_general(
         grad_attn_proj, full_out, (((1,), (1,)), ((), ())), preferred_element_type=jnp.float32
     ).astype(jnp.bfloat16)
@@ -552,9 +645,6 @@
     grad_key_raw, grad_gain_key = pullback(grad_keys[:, None, :])
     grad_query_raw = grad_query_raw.reshape(row_count, head_count * head_dim).astype(jnp.bfloat16)
     grad_key_raw = grad_key_raw[:, 0].astype(jnp.bfloat16)
-    grad_w_query = weight_grad(normed_in, grad_query_raw)
-    grad_w_key = weight_grad(normed_in, grad_key_raw)
-    grad_w_value = weight_grad(normed_in, grad_values)
     grad_normed_in = lax.dot_general(
         grad_query_raw, full_query, (((1,), (1,)), ((), ())), preferred_element_type=jnp.float32
     )
@@ -567,40 +657,18 @@
     _, pullback = jax.vjp(rms_gain, x_float, in_gain)
     grad_input_part, grad_gain_in = pullback(grad_normed_in)
     grad_inputs = grad_resid + grad_input_part
-    attn_gradients = (
-        grad_w_query,
-        grad_w_key,
-        grad_w_value,
-        grad_w_out,
-        grad_gain_in,
-        grad_gain_attn_post,
-        grad_gain_query,
-        grad_gain_key,
-    )
-    depth = lax.axis_size("seq") // 4
-    bf16 = [g.astype(jnp.bfloat16) for g in attn_gradients[:4] + ff_gradients[:3]]
-    by_columns = [
-        bf16[4], bf16[5], bf16[0], jnp.concatenate([bf16[1], bf16[2]], axis=1)
-    ]
-    pieces = [split_columns(g, depth) for g in by_columns]
-    piece_rows = pieces[0].shape[5]
-    by_rows = [bf16[6], bf16[3]]
-    pieces = pieces[:2] + [split_rows(by_rows[0], depth, piece_rows)] + pieces[2:]
-    pieces = pieces + [split_rows(by_rows[1], depth, piece_rows)]
-    gain_terms = attn_gradients[4:6] + ff_gradients[3:5] + attn_gradients[6:8]
+    keys_values = jnp.concatenate([grad_key_raw, grad_values], axis=1)
+    lefts = (normed_ff, normed_ff, hidden, normed_in, normed_in, attended)
+    rights = (grad_gate, grad_up, grad_ff_proj, grad_query_raw, keys_values, grad_attn_proj)
+    gain_terms = (
+        grad_gain_in, grad_gain_attn_post, grad_gain_ff_pre, grad_gain_ff_post,
+        grad_gain_query, grad_gain_key,
+    )
     gain_rows = jnp.concatenate(gain_terms).astype(jnp.bfloat16).astype(jnp.float32)
-    summed, gain_sums = reduce_terms(
-        jnp.concatenate(pieces, axis=0), gain_rows.reshape(-1, LANES)
-    )
-    bounds = [0]
-    for piece in pieces:
-        bounds.append(bounds[-1] + piece.shape[0])
-    cuts = [summed[low:high].astype(jnp.float32) for low, high in zip(bounds[:-1], bounds[1:])]
-    sum_gate, sum_up, sum_query, sum_key_value = [
-        join_columns(cuts[i]) for i in (0, 1, 3, 4)
-    ]
-    sum_down = join_rows(cuts[2], by_rows[0].shape[1])
-    sum_out = join_rows(cuts[5], by_rows[1].shape[1])
+    summed, gain_sums = reduce_terms(lefts, rights, gain_rows.reshape(-1, LANES))
+    sum_gate, sum_up, sum_down, sum_query, sum_key, sum_value, sum_out = unpack(
+        summed, [w.shape for w in (w_gate, w_up, w_down, w_query, w_key, w_value, w_out)]
+    )
     me = lax.axis_index("wshard")
     gain_sums = gain_sums[3].reshape(-1)
     gain_outs = []
@@ -610,8 +678,7 @@
         gain_outs.append(lax.dynamic_slice_in_dim(gain_sums, start + me * half, half))
         start += term.shape[0]
     return (
-        layer_out, grad_inputs, sum_query, sum_key_value[:, :head_dim], sum_key_value[:, head_dim:],
-        sum_out, sum_gate, sum_up, sum_down,
+        layer_out, grad_inputs, sum_query, sum_key, sum_value, sum_out, sum_gate, sum_up, sum_down,
     ) + tuple(gain_outs)
 
 

time: 372 us -> 298 us (0.80); the launches traced: 366 us -> 296 us
  local copies, waits for them, and re-layouts: 104 us -> 27 us
  Pallas kernels: 152 us -> 164 us
  matrix products: 53.6 us -> 47.5 us
    reshape x16 -> x1, local copies, waits for them, and re-layouts: 53.7 us -> 1.24 us  [per_device(): grad_heads = grad_attended.reshape(row_count, head_count, head_dim)]
    unnamed x126 -> x108, local copies, waits for them, and re-layouts: 26 us -> 9.65 us
    pallas_call x1 -> x2, Pallas kernels: 104 us -> 115 us  [the longest x1 102 us: reduce_terms(): pl.pallas_call(functools.partial(reduce_kernel, len(lefts)), out_shape=[j...]
    dot_general x7 -> x0, matrix products: 11.3 us -> none  [weight_grad(): jnp.einsum('tc,tf->cf', left_rows, right_rows, preferred_element_type=jnp...]
    transpose x2 -> x0, local copies, waits for them, and re-layouts: 7.53 us -> none  [split_rows(): term = term.transpose(1, 2, 0, 3, 4, 6, 5, 7)]
    slice x2 -> x0, other arithmetic: 4.08 us -> none  [per_device(): summed[low:high].astype(jnp.float32)]
  transfers between devices with their start and end apart: 10 -> 10, of which waited for: 0 -> 1; matrix products, arithmetic and copies ran while one was open for 24% -> 14% of each run, Pallas kernels for 0% -> 0%
where the time goes in v2:
time: 298 us; the launch traced here: 296 us
  Pallas kernels  164 us (55%)
  matrix products  47.5 us (16%)
  other arithmetic  30.9 us (10%)
  local copies, waits for them, and re-layouts  27 us (9%)
  starting transfers between devices  22.5 us (8%)
    pallas_call x1, Pallas kernels, reduce_terms(): pl.pallas_call(functools.partial(reduce_kernel, len(lefts)), out_shape=[j...  102 us
    pallas_call x1, Pallas kernels, gather_weights(): pl.pallas_call(functools.partial(gather_kernel, count), out_shape=[jax.Sh...  48.6 us
    ppermute x10, starting transfers between devices, from_behind(): return lax.ppermute(array, axis, pairs)  22.5 us
    pallas_call x1, Pallas kernels, unpack(): pl.pallas_call(functools.partial(unpack_kernel, plan), grid=(chunks,), ou...  13.5 us
    unnamed x108, local copies, waits for them, and re-layouts  9.65 us
    dot_general x1, matrix products, per_device(): jnp.einsum('hqk,kd->qhd', grad_score, all_keys, preferred_element_type=jn...  8.27 us
    dot_general x1, matrix products, per_device(): jnp.einsum('hqk,qhd->kd', grad_score, queries, preferred_element_type=jnp...  7.86 us
  transfers between devices with their start and end apart: 10, of which 1 were waited for; matrix products, arithmetic and copies ran while one was open for 14% of the time, Pallas kernels for 0%

profile of v2, /device:TPU:0, one launch (start us, length us, event | category | flops | bytes accessed | tf_op | source)
XLA Modules:
  0.0 296.2 jit_solution(9318817381783140639)
XLA Ops:
  0.6 4.2 %concatenate.27 = bf16[1536]{0:T(1024)(128)(2,1)S(1)} concatenate(bf16[320]{0:T(512)(128)(2,1)} %param.25, bf16[320]{0:T(512)(128)(2,1)} %param.26, bf16[320]{0:T(512)(128)(2,1)} %param.27, bf16[320]{0:T(512)(128)(2,1)} %param.28, bf16[128]{0:T(256)(128)(2,1)} %param.29, bf16[128]{0:T(256)(128)(2,1)} %param.30), dimensions={0} | concatenate | bytes 6144 | tf_op jit(solution)/shard_map/concatenate | solution.py:508
  8.8 48.6 %gather_weights.1 = (bf16[640,1024]{1,0:T(8,128)(2,1)S(1)}, bf16[640,256]{1,0:T(8,128)(2,1)S(1)}, bf16[640,256]{1,0:T(8,128)(2,1)S(1)}, bf16[1024,640]{1,0:T(8,1...) custom-call(bf16[320,1024]{1,0:T(8,128)(2,1)S(1)} %copy-done, ...), custom_call_target="tpu_custom_call" | custom-call | tf_op jit(solution)/shard_map/gather_weights/pallas_call | solution.py:168
  62.1 3.2 %collective-permute-start.1 = (bf16[256,256]{1,0:T(8,128)(2,1)}, bf16[256,256]{1,0:T(8,128)(2,1)}, u32[]{:S(2)}, u32[]{:S(2)}) collective-permute-start(bf16[256,256]{1,0:T(8,128)(2,1)} %convolution_convert_fusion.2), channel_id=1, source_target_pairs={{0,1},{1,2},{2,3},{3,4},{4,5},{5,6},{6,7},{7,8},{8,9},{9,10},{10,1... | collective-permute-start | bytes 393224 | tf_op jit(solution)/shard_map/ppermute | solution.py:21
  65.3 2.0 collective-permute-start
  67.4 3.9 %collective-permute-start.3 = (s32[256]{0:T(256)}, s32[256]{0:T(256)}, u32[]{:S(2)}, u32[]{:S(2)}) collective-permute-start(s32[256]{0:T(256)} %param.17), channel_id=1, source_target_pairs={{0,1},{1,2},{2,3},{3,4},{4,5},{5,6},{6,7},{7,8},{8,9},{9,10},{10,1... | collective-permute-start | bytes 3080 | tf_op jit(solution)/shard_map/ppermute | solution.py:21
  71.3 1.8 collective-permute-start.2
  74.2 2.6 multiply_reduce_fusion.9
  81.1 2.7 collective-permute-start.5
  85.5 1.9 multiply_cosine_fusion
  87.5 2.5 fusion.85
  90.0 2.7 reshape.443
  92.7 2.2 multiply_reduce_fusion.1
  98.6 1.4 fusion.19
  100.1 1.9 subtract_convert_fusion
  102.0 3.3 %collective-permute-start.4 = (bf16[256,256]{1,0:T(8,128)(2,1)}, bf16[256,256]{1,0:T(8,128)(2,1)S(1)}, u32[]{:S(2)}, u32[]{:S(2)}) collective-permute-start(bf16[256,256]{1,0:T(8,128)(2,1)} %maximum_bitcast_fusion.6), channel_id=1, source_target_pairs={{0,2},{1,3},{2,4},{3,5},{4,6},{5,7},{6,8},{7,9},{8,10},{9,11},{10,... | collective-permute-start | bytes 393224 | tf_op jit(solution)/shard_map/ppermute | solution.py:21
  106.0 1.6 fusion.24
  107.7 1.9 fusion.4
  110.5 3.1 %convolution_convert_fusion.1 = bf16[256,4,256]{2,0,1:T(8,128)(2,1)} fusion(bf16[256,256]{1,0:T(8,128)(2,1)} %convolution_convert_fusion.2, bf16[256,256]{1,0:T(8,128)(2,1)} %collective-permute-done.1, bf16[256,256]{1,0:T(8,128)(2,1)} %collective-permute-done, f32[768,256,4]{1,0,2:T(8,128)S(1)} %get-tuple-element.97, f32[4,256]{1,0:T(4,128)S(1)} %log_add_fusion, ...), kind=kOutput, calls=%fused_computation.35 | convolution fusion | flops 408027136 | bytes 4263936 | tf_op jit(solution)/shard_map/hqk,kd->qhd/dot_general | solution.py:559
  113.5 2.0 copy.159.refs_5_
  115.6 1.9 multiply_reduce_fusion.8
  125.2 2.5 multiply_convert_fusion
  128.8 1.7 multiply_reduce_fusion.2
  133.1 1.4 convolution_convert_fusion
  135.7 3.9 %fusion.84 = (bf16[768,256]{1,0:T(8,128)(2,1)}, f32[768,256]{1,0:T(8,128)}) fusion(bf16[256,4,256]{0,2,1:T(8,128)(2,1)S(1)} %bitcast.186, f32[4,256]{1,0:T(4,128)S(1)} %copy-done.47, f32[768,256,4]{1,0,2:T(8,128)} %copy-done.12, pred[256,768]{0,1:T(8,128)(4,1)} %copy-done.22), kind=kOutput, calls=%fused_computation.180 | convolution fusion | flops 406781952 | bytes 5050368 | tf_op jit(solution)/shard_map/hqk,qhd->kd/dot_general | solution.py:609
  139.7 3.3 %fusion.45 = f32[768,256,4]{1,0,2:T(8,128)} fusion(bf16[256,4,256]{0,2,1:T(8,128)(2,1)S(1)} %bitcast.187, bf16[256,256]{1,0:T(8,128)(2,1)} %convolution_convert_fusion.2, bf16[256,256]{1,0:T(8,128)(2,1)} %collective-permute-done.1, bf16[256,256]{1,0:T(8,128)(2,1)} %collective-permute-done), kind=kOutput, calls=%fused_computation.108 | convolution fusion | flops 403832832 | bytes 4063232 | tf_op jit(solution)/shard_map/qhd,kd->hqk/dot_general | solution.py:598
  143.0 7.9 %fusion.83 = (bf16[768,256]{1,0:T(8,128)(2,1)S(1)}, f32[768,256]{1,0:T(8,128)}) fusion(bf16[256,4,128]{2,0,1:T(8,128)(2,1)S(1)} %copy-done.24, bf16[256,4,128]{2,0,1:T(8,128)(2,1)S(1)} %copy-done.23, f32[768,256,4]{1,0,2:T(8,128)} %fusion.45, f32[4,256]{1,0:T(4,128)S(1)} %copy-done.47, f32[768,256,4]{1,0,2:T(8,128)} %copy-done.12, ...), kind=kOutput, calls=%fused_computation.179 | convolution fusion | flops 414123776 | bytes 8196096 | tf_op jit(solution)/shard_map/hqk,qhd->kd/dot_general | solution.py:606
  152.9 1.4 collective-permute-start.6
  154.4 8.3 %fusion.15 = f32[256,4,256]{2,0,1:T(8,128)} fusion(f32[768,256,4]{1,0,2:T(8,128)} %fusion.45, bf16[256,256]{1,0:T(8,128)(2,1)} %maximum_bitcast_fusion.6, bf16[256,256]{1,0:T(8,128)(2,1)} %collective-permute-done.5, bf16[256,256]{1,0:T(8,128)(2,1)} %copy-done.50, f32[768,256,4]{1,0,2:T(8,128)} %copy-done.12, f32[4,256]{1,0:T(4,128)S(1)} %copy-done.48, ...), kind=kOutput, calls=%fused_computation.26 | convolution fusion | flops 414058240 | bytes 7933952 | tf_op jit(solution)/shard_map/hqk,kd->qhd/dot_general | solution.py:603
  166.3 1.6 collective-permute-start.8
  170.2 2.7 collective-permute-done.9
  177.7 102.0 %reduce_terms.1 = (bf16[17,2,2,4,80,128]{5,4,3,2,1,0:T(8,128)(2,1)}, f32[4,24,128]{2,1,0:T(8,128)}) custom-call(bf16[256,640]{1,0:T(8,128)(2,1)} %copy-done.9, bf16[256,640]{1,0:T(8,128)(2,1)} %copy-done.9, bf16[256,2048]{1,0:T(8,128)(2,1)} %copy-done.20, bf16[256,640]{1,0:T(8,128)(2,1)} %copy-done.5, bf16[256,640]{1,0:T(8,128)(2,1)} %copy-done.5, ...), custom_call_target="tpu_custom_call" | custom-call | tf_op jit(solution)/shard_map/reduce_terms/pallas_call | solution.py:402
  279.7 13.5 %unpack.1 = (f32[320,2048]{1,0:T(8,128)}, f32[320,2048]{1,0:T(8,128)}, f32[1024,640]{1,0:T(8,128)}, f32[320,1024]{1,0:T(8,128)}, f32[320,256]{1,0:T(8,128)}, /*index=5*/f32[320,256]{1,0:T(8,128)}, f32[512,640]{1,0:T(8,128)}) custom-call(bf16[17,2,2,4,80,128]{5,4,3,2,1,0:T(8,128)(2,1)} %get-tuple-element.40.summed), custom_call_target="tpu_custom_call" | custom-call | tf_op jit(solution)/shard_map/unpack/pallas_call | solution.py:479
  (187 shorter events, 49.2 us)
Async XLA Ops:
  59.3 13.7 %copy-start.38 = (f32[256]{0:T(256)}, f32[256]{0:T(256)S(1)}, u32[]{:S(2)}) copy-start(f32[256]{0:T(256)S(1)} %fusion.36) | copy-start | bytes 3076
  59.3 17.4 %copy-start.29 = (f32[256]{0:T(256)}, f32[256]{0:T(256)S(1)}, u32[]{:S(2)}) copy-start(f32[256]{0:T(256)S(1)} %fusion.64) | copy-start | bytes 3076
  62.1 48.3 %collective-permute-start.1 = (bf16[256,256]{1,0:T(8,128)(2,1)}, bf16[256,256]{1,0:T(8,128)(2,1)}, u32[]{:S(2)}, u32[]{:S(2)}) collective-permute-start(bf16[256,256]{1,0:T(8,128)(2,1)} %convolution_convert_fusion.2), channel_id=1, source_target_pairs={{0,1},{1,2},{2,3},{3,4},{4,5},{5,6},{6,7},{7,8},{8,9},{9,10},{10,1... | collective-permute-start | bytes 393224 | tf_op jit(solution)/shard_map/ppermute | solution.py:21
  65.3 45.1 %collective-permute-start = (bf16[256,256]{1,0:T(8,128)(2,1)}, bf16[256,256]{1,0:T(8,128)(2,1)}, u32[]{:S(2)}, u32[]{:S(2)}) collective-permute-start(bf16[256,256]{1,0:T(8,128)(2,1)} %convolution_convert_fusion.2), channel_id=1, source_target_pairs={{0,2},{1,3},{2,4},{3,5},{4,6},{5,7},{6,8},{7,9},{8,10},{9,11},{10,... | collective-permute-start | bytes 393224 | tf_op jit(solution)/shard_map/ppermute | solution.py:21
  67.4 34.6 %collective-permute-start.3 = (s32[256]{0:T(256)}, s32[256]{0:T(256)}, u32[]{:S(2)}, u32[]{:S(2)}) collective-permute-start(s32[256]{0:T(256)} %param.17), channel_id=1, source_target_pairs={{0,1},{1,2},{2,3},{3,4},{4,5},{5,6},{6,7},{7,8},{8,9},{9,10},{10,1... | collective-permute-start | bytes 3080 | tf_op jit(solution)/shard_map/ppermute | solution.py:21
  71.3 34.0 %collective-permute-start.2 = (s32[256]{0:T(256)}, s32[256]{0:T(256)}, u32[]{:S(2)}, u32[]{:S(2)}) collective-permute-start(s32[256]{0:T(256)} %param.17), channel_id=1, source_target_pairs={{0,2},{1,3},{2,4},{3,5},{4,6},{5,7},{6,8},{7,9},{8,10},{9,11},{10,... | collective-permute-start | bytes 3080 | tf_op jit(solution)/shard_map/ppermute | solution.py:21
  73.6 13.8 %copy-start.33 = (f32[256]{0:T(256)}, f32[256]{0:T(256)S(1)}, u32[]{:S(2)}) copy-start(f32[256]{0:T(256)S(1)} %get-tuple-element.90) | copy-start | bytes 3076
  74.2 18.6 %copy-start.36 = (f32[256]{0:T(256)}, f32[256]{0:T(256)S(1)}, u32[]{:S(2)}) copy-start(f32[256]{0:T(256)S(1)} %fusion.71) | copy-start | bytes 3076
  81.1 26.5 %collective-permute-start.5 = (bf16[256,256]{1,0:T(8,128)(2,1)}, bf16[256,256]{1,0:T(8,128)(2,1)}, u32[]{:S(2)}, u32[]{:S(2)}) collective-permute-start(bf16[256,256]{1,0:T(8,128)(2,1)} %maximum_bitcast_fusion.6), channel_id=1, source_target_pairs={{0,1},{1,2},{2,3},{3,4},{4,5},{5,6},{6,7},{7,8},{8,9},{9,10},{10,1... | collective-permute-start | bytes 393224 | tf_op jit(solution)/shard_map/ppermute | solution.py:21
  102.0 5.7 %collective-permute-start.4 = (bf16[256,256]{1,0:T(8,128)(2,1)}, bf16[256,256]{1,0:T(8,128)(2,1)S(1)}, u32[]{:S(2)}, u32[]{:S(2)}) collective-permute-start(bf16[256,256]{1,0:T(8,128)(2,1)} %maximum_bitcast_fusion.6), channel_id=1, source_target_pairs={{0,2},{1,3},{2,4},{3,5},{4,6},{5,7},{6,8},{7,9},{8,10},{9,11},{10,... | collective-permute-start | bytes 393224 | tf_op jit(solution)/shard_map/ppermute | solution.py:21
  109.6 3.9 %copy-start.12 = (f32[768,256,4]{1,0,2:T(8,128)}, f32[768,256,4]{1,0,2:T(8,128)S(1)}, u32[]{:S(2)}) copy-start(f32[768,256,4]{1,0,2:T(8,128)S(1)} %get-tuple-element.97) | copy-start | bytes 9437188
  131.5 4.2 %copy-start.47 = (f32[4,256]{1,0:T(4,128)S(1)}, f32[4,256]{1,0:T(4,128)}, u32[]{:S(2)}) copy-start(f32[4,256]{1,0:T(4,128)} %copy-done.46) | copy-start | bytes 12292
  143.0 11.3 %copy-start.48 = (f32[4,256]{1,0:T(4,128)S(1)}, f32[4,256]{1,0:T(4,128)}, u32[]{:S(2)}) copy-start(f32[4,256]{1,0:T(4,128)} %copy-done.46) | copy-start | bytes 12292
  151.6 16.3 %collective-permute-start.7 = (bf16[256,256]{1,0:T(8,128)(2,1)}, bf16[256,256]{1,0:T(8,128)(2,1)}, u32[]{:S(2)}, u32[]{:S(2)}) collective-permute-start(bf16[256,256]{1,0:T(8,128)(2,1)} %get-tuple-element.75), channel_id=1, source_target_pairs={{1,0},{2,1},{3,2},{4,3},{5,4},{6,5},{7,6},{8,7},{9,8},{10,9},{11,1... | collective-permute-start | bytes 393224 | tf_op jit(solution)/shard_map/ppermute | solution.py:21
  152.9 9.8 %copy-start.18 = (f32[256,128]{1,0:T(8,128)S(1)}, f32[256,128]{1,0:T(8,128)}, u32[]{:S(2)}) copy-start(f32[256,128]{1,0:T(8,128)} %get-tuple-element.92) | copy-start | bytes 393220
  152.9 9.7 %copy-start.19 = (f32[256,128]{1,0:T(8,128)S(1)}, f32[256,128]{1,0:T(8,128)}, u32[]{:S(2)}) copy-start(f32[256,128]{1,0:T(8,128)} %get-tuple-element.93) | copy-start | bytes 393220
  152.9 11.1 %copy-start.4 = (f32[256,1024]{1,0:T(8,128)S(1)}, f32[256,1024]{1,0:T(8,128)}, u32[]{:S(2)}) copy-start(f32[256,1024]{1,0:T(8,128)} %fusion.85) | copy-start | bytes 3145732
  152.9 11.1 %copy-start.35 = (f32[256]{0:T(256)S(1)}, f32[256]{0:T(256)}, u32[]{:S(2)}) copy-start(f32[256]{0:T(256)} %get-tuple-element.91) | copy-start | bytes 3076
  152.9 15.0 %collective-permute-start.6 = (bf16[256,256]{1,0:T(8,128)(2,1)}, bf16[256,256]{1,0:T(8,128)(2,1)}, u32[]{:S(2)}, u32[]{:S(2)}) collective-permute-start(bf16[256,256]{1,0:T(8,128)(2,1)} %get-tuple-element.74), channel_id=1, source_target_pairs={{2,0},{3,1},{4,2},{5,3},{6,4},{7,5},{8,6},{9,7},{10,8},{11,9},{12,... | collective-permute-start | bytes 393224 | tf_op jit(solution)/shard_map/ppermute | solution.py:21
  164.0 5.0 %copy-start.37 = (f32[256]{0:T(256)S(1)}, f32[256]{0:T(256)}, u32[]{:S(2)}) copy-start(f32[256]{0:T(256)} %copy-done.36) | copy-start | bytes 3076
  164.0 5.0 %copy-start.45 = (f32[128]{0:T(128)S(1)}, f32[128]{0:T(128)}, u32[]{:S(2)}) copy-start(f32[128]{0:T(128)} %multiply_exponential_fusion) | copy-start | bytes 1540
  164.5 5.1 %copy-start.32 = (f32[256]{0:T(256)S(1)}, f32[256]{0:T(256)}, u32[]{:S(2)}) copy-start(f32[256]{0:T(256)} %copy-done.31) | copy-start | bytes 3076
  164.5 5.1 %copy-start.34 = (f32[256]{0:T(256)S(1)}, f32[256]{0:T(256)}, u32[]{:S(2)}) copy-start(f32[256]{0:T(256)} %copy-done.33) | copy-start | bytes 3076
  164.5 5.3 %copy-start.40 = (f32[256]{0:T(256)S(1)}, f32[256]{0:T(256)}, u32[]{:S(2)}) copy-start(f32[256]{0:T(256)} %get-tuple-element.94) | copy-start | bytes 3076
  165.0 10.4 %copy-start.10 = (bf16[4,32,8,256]{3,2,0,1:T(8,128)(2,1)}, bf16[4,32,8,256]{3,2,0,1:T(8,128)(2,1)S(1)}, u32[]{:S(2)}) copy-start(bf16[4,32,8,256]{3,2,0,1:T(8,128)(2,1)S(1)} %copy.167) | copy-start | bytes 1572868
  165.0 7.9 %collective-permute-start.9 = (bf16[256,256]{1,0:T(8,128)(2,1)S(1)}, bf16[256,256]{1,0:T(8,128)(2,1)S(1)}, u32[]{:S(2)}, u32[]{:S(2)}) collective-permute-start(bf16[256,256]{1,0:T(8,128)(2,1)S(1)} %get-tuple-element.73), channel_id=1, source_target_pairs={{1,0},{2,1},{3,2},{4,3},{5,4},{6,5},{7,6},{8,7},{9,8},{10,9},{11,1... | collective-permute-start | bytes 393224 | tf_op jit(solution)/shard_map/ppermute | solution.py:21
  166.3 6.6 %collective-permute-start.8 = (bf16[256,256]{1,0:T(8,128)(2,1)S(1)}, bf16[256,256]{1,0:T(8,128)(2,1)S(1)}, u32[]{:S(2)}, u32[]{:S(2)}) collective-permute-start(bf16[256,256]{1,0:T(8,128)(2,1)S(1)} %get-tuple-element.72), channel_id=1, source_target_pairs={{2,0},{3,1},{4,2},{5,3},{6,4},{7,5},{8,6},{9,7},{10,8},{11,9},{12,... | collective-permute-start | bytes 393224 | tf_op jit(solution)/shard_map/ppermute | solution.py:21
  169.8 5.6 %copy-start.6 = (bf16[256,640]{1,0:T(8,128)(2,1)S(1)}, bf16[256,640]{1,0:T(8,128)(2,1)}, u32[]{:S(2)}) copy-start(bf16[256,640]{1,0:T(8,128)(2,1)} %param.16) | copy-start | bytes 983044
  169.8 5.6 %copy-start.30 = (f32[256]{0:T(256)S(1)}, f32[256]{0:T(256)}, u32[]{:S(2)}) copy-start(f32[256]{0:T(256)} %copy-done.29) | copy-start | bytes 3076
  172.9 3.4 %copy-start.42 = (bf16[640]{0:T(1024)(128)(2,1)S(1)}, bf16[640]{0:T(1024)(128)(2,1)}, u32[]{:S(2)}) copy-start(bf16[640]{0:T(1024)(128)(2,1)} %get-tuple-element.51) | copy-start | bytes 3844
  172.9 3.6 %copy-start.41 = (bf16[640]{0:T(1024)(128)(2,1)S(1)}, bf16[640]{0:T(1024)(128)(2,1)}, u32[]{:S(2)}) copy-start(bf16[640]{0:T(1024)(128)(2,1)} %get-tuple-element.55) | copy-start | bytes 3844
  279.7 14.2 %copy-start.8 = (f32[256,640]{1,0:T(8,128)S(1)}, f32[256,640]{1,0:T(8,128)}, u32[]{:S(2)}) copy-start(f32[256,640]{1,0:T(8,128)} %copy-done.7) | copy-start | bytes 1966084
  (29 other events, 58.3 us)

commit v3 on v2

--- a/solution.py
+++ b/solution.py
@@ -176,7 +176,7 @@
             pltpu.SemaphoreType.DMA((3, count)),
         ],
         compiler_params=pltpu.CompilerParams(
-            collective_id=1, has_side_effects=True, vmem_limit_bytes=48 * 2**20
+            collective_id=1, has_side_effects=True, vmem_limit_bytes=58 * 2**20
         ),
         name="gather_weights",
     )(*shards)
@@ -486,6 +486,77 @@
     )(summed)
 
 
+def shift_kernel(count, hops, step, *refs):
+    arrays, outs = refs[:count], refs[count : 2 * count]
+    send_sems, recv_sems = refs[2 * count :]
+    width = lax.axis_size("wshard")
+    total = lax.axis_size("seq") * width
+    me = lax.axis_index("seq") * width + lax.axis_index("wshard")
+    barrier = pltpu.get_barrier_semaphore()
+    offsets = [d for d in range(-hops, hops + 1) if d != 0]
+
+    def there(offset):
+        return (me + offset >= 0) & (me + offset < total)
+
+    def target(offset):
+        place = lax.rem(me + offset + total, total)
+        return (place // width, lax.rem(place, width))
+
+    for offset in offsets:
+        pl.semaphore_signal(
+            barrier, inc=1, device_id=target(offset), device_id_type=MESH
+        )
+    pl.semaphore_wait(barrier, len(offsets))
+
+    def copy(k, d):
+        source = arrays[k] if step > 0 else arrays[k].at[hops - d]
+        return remote(
+            source, outs[k].at[d - 1], send_sems.at[k, d - 1], recv_sems.at[k, d - 1],
+            target(step * d),
+        )
+
+    for d in range(1, hops + 1):
+        @pl.when(there(step * d))
+        def _():
+            for k in range(count):
+                copy(k, d).start()
+    for d in range(1, hops + 1):
+        @pl.when(there(-step * d))
+        def _():
+            for k in range(count):
+                copy(k, d).wait_recv()
+
+        @pl.when(jnp.logical_not(there(-step * d)))
+        def _():
+            for k in range(count):
+                outs[k][d - 1] = jnp.zeros(outs[k].shape[1:], outs[k].dtype)
+    for d in range(1, hops + 1):
+        @pl.when(there(step * d))
+        def _():
+            for k in range(count):
+                copy(k, d).wait_send()
+
+
+def shift(arrays, hops, step, name, collective_id):
+    count = len(arrays)
+    vmem = pl.BlockSpec(memory_space=pltpu.VMEM)
+    shapes = [a.shape if step > 0 else a.shape[1:] for a in arrays]
+    return pl.pallas_call(
+        functools.partial(shift_kernel, count, hops, step),
+        out_shape=[
+            jax.ShapeDtypeStruct((hops,) + s, a.dtype) for s, a in zip(shapes, arrays)
+        ],
+        in_specs=[vmem] * count,
+        out_specs=[vmem] * count,
+        scratch_shapes=[
+            pltpu.SemaphoreType.DMA((count, hops)),
+            pltpu.SemaphoreType.DMA((count, hops)),
+        ],
+        compiler_params=pltpu.CompilerParams(collective_id=collective_id, has_side_effects=True),
+        name=name,
+    )(*arrays)
+
+
 def per_device(
     inputs,
     doc_ids,
@@ -535,15 +606,13 @@
     key_rot = norm_rope(key_raw, key_gain, cos_table, sin_table)[:, 0].astype(jnp.bfloat16)
     sent_rows = min(WINDOW, row_count)
     hop_count = WINDOW // sent_rows
-    outgoing = (key_rot, values, doc_ids)
-    halo_keys = []
-    halo_values = []
-    halo_docs = []
-    for distance in range(hop_count, 0, -1):
-        arrived = from_behind((outgoing[0], outgoing[1], outgoing[2]), ("seq", "wshard"), distance)
-        halo_keys.append(arrived[0])
-        halo_values.append(arrived[1])
-        halo_docs.append(arrived[2])
+    arrived = shift(
+        (key_rot, values, doc_ids.reshape(-1, LANES)), hop_count, 1, "shift_on", 3
+    )
+    order = range(hop_count - 1, -1, -1)
+    halo_keys = [arrived[0][i] for i in order]
+    halo_values = [arrived[1][i] for i in order]
+    halo_docs = [arrived[2][i].reshape(-1) for i in order]
     all_keys = jnp.concatenate(halo_keys + [key_rot], 0)
     all_values = jnp.concatenate(halo_values + [values], 0)
     all_docs = jnp.concatenate(halo_docs + [doc_ids], 0)
@@ -609,25 +678,15 @@
     grad_values_all = jnp.einsum(
         "hqk,qhd->kd", probs.astype(jnp.bfloat16), grad_heads, preferred_element_type=jnp.float32
     )
-    back_keys = jnp.zeros((sent_rows, head_dim), jnp.float32)
-    back_values = jnp.zeros((sent_rows, head_dim), jnp.float32)
-    for piece_index in range(hop_count):
-        distance = hop_count - piece_index
-        piece_start = piece_index * sent_rows
-        arrived = (
-            from_behind(
-                grad_keys_all[piece_start : piece_start + sent_rows].astype(jnp.bfloat16),
-                ("seq", "wshard"),
-                -distance,
-            ).astype(jnp.float32),
-            from_behind(
-                grad_values_all[piece_start : piece_start + sent_rows].astype(jnp.bfloat16),
-                ("seq", "wshard"),
-                -distance,
-            ).astype(jnp.float32),
-        )
-        back_keys = back_keys + arrived[0]
-        back_values = back_values + arrived[1]
+    pieces = (hop_count, sent_rows, head_dim)
+    returned = shift(
+        (
+            grad_keys_all[:WINDOW].astype(jnp.bfloat16).reshape(pieces),
+            grad_values_all[:WINDOW].astype(jnp.bfloat16).reshape(pieces),
+        ),
+        hop_count, -1, "shift_back", 4,
+    )
+    back_keys, back_values = [jnp.sum(r.astype(jnp.float32), axis=0) for r in returned]
     own_keys = grad_keys_all[WINDOW:]
     own_values = grad_values_all[WINDOW:]
     split_row = row_count - sent_rows

time: 298 us -> 273 us (0.916)
  starting transfers between devices: 22.5 us -> 0 us
  Pallas kernels: 164 us -> 183 us
  other arithmetic: 30.9 us -> 19.5 us
  local copies, waits for them, and re-layouts: 27 us -> 22 us
    ppermute x10 -> x0, starting transfers between devices: 22.5 us -> none  [from_behind(): return lax.ppermute(array, axis, pairs)]
    pallas_call x0 -> x2, Pallas kernels: none -> 21.5 us  [shift(): pl.pallas_call(functools.partial(shift_kernel, count, hops, step), out_sh...]
    pallas_call x1, Pallas kernels: 102 us -> 98.1 us  [reduce_terms(): pl.pallas_call(functools.partial(reduce_kernel, len(lefts)), out_shape=[j...]
    reduce_sum x3, other arithmetic: 4.61 us -> 0.79 us  [rms_gain(): jnp.mean(tensor * tensor, axis=-1, keepdims=True) + NORM_EPSILON]
    unnamed x108 -> x110, local copies, waits for them, and re-layouts: 9.65 us -> 8.67 us
  transfers between devices with their start and end apart: 10 -> 0, of which waited for: 1 -> 0; matrix products, arithmetic and copies ran while one was open for 14% -> 0% of each run, Pallas kernels for 0% -> 0%
where the time goes in v3:
time: 273 us; the launch traced here: 271 us
  Pallas kernels  183 us (67%)
  matrix products  45.7 us (17%)
  local copies, waits for them, and re-layouts  22 us (8%)
  other arithmetic  19.5 us (7%)
    pallas_call x1, Pallas kernels, reduce_terms(): pl.pallas_call(functools.partial(reduce_kernel, len(lefts)), out_shape=[j...  98.1 us
    pallas_call x1, Pallas kernels, gather_weights(): pl.pallas_call(functools.partial(gather_kernel, count), out_shape=[jax.Sh...  49.7 us
    pallas_call x2, Pallas kernels, shift(): pl.pallas_call(functools.partial(shift_kernel, count, hops, step), out_sh...  21.5 us
    pallas_call x1, Pallas kernels, unpack(): pl.pallas_call(functools.partial(unpack_kernel, plan), grid=(chunks,), ou...  13.5 us
    unnamed x110, local copies, waits for them, and re-layouts  8.67 us
    dot_general x1, matrix products, per_device(): jnp.einsum('hqk,kd->qhd', grad_score, all_keys, preferred_element_type=jn...  8.3 us
    dot_general x1, matrix products, per_device(): jnp.einsum('hqk,qhd->kd', grad_score, queries, preferred_element_type=jnp...  7.8 us

profile of v3, /device:TPU:0, one launch (start us, length us, event | category | flops | bytes accessed | tf_op | source)
XLA Modules:
  0.0 271.5 jit_solution(8852543411733701327)
XLA Ops:
  0.7 4.2 %concatenate.27 = bf16[1536]{0:T(1024)(128)(2,1)S(1)} concatenate(bf16[320]{0:T(512)(128)(2,1)} %param.25, bf16[320]{0:T(512)(128)(2,1)} %param.26, bf16[320]{0:T(512)(128)(2,1)} %param.27, bf16[320]{0:T(512)(128)(2,1)} %param.28, bf16[128]{0:T(256)(128)(2,1)} %param.29, bf16[128]{0:T(256)(128)(2,1)} %param.30), dimensions={0} | concatenate | bytes 6144 | tf_op jit(solution)/shard_map/concatenate | solution.py:579
  5.5 49.7 %gather_weights.1 = (bf16[640,1024]{1,0:T(8,128)(2,1)}, bf16[640,256]{1,0:T(8,128)(2,1)}, bf16[640,256]{1,0:T(8,128)(2,1)}, bf16[1024,640]{1,0:T(8,128)(2,1)}, b...) custom-call(bf16[320,1024]{1,0:T(8,128)(2,1)} %refs_0_.1, ...), custom_call_target="tpu_custom_call" | custom-call | tf_op jit(solution)/shard_map/gather_weights/pallas_call | solution.py:168
  56.6 2.0 convolution_convert_fusion.2.refs_1_
  58.7 1.3 multiply_reduce_fusion.9
  61.5 9.5 %shift_on.1 = (bf16[2,256,256]{2,1,0:T(8,128)(2,1)}, bf16[2,256,256]{2,1,0:T(8,128)(2,1)}, s32[2,2,128]{2,1,0:T(2,128)}) custom-call(bf16[256,256]{1,0:T(8,128)(2,1)} %maximum_bitcast_fusion.6.refs_0_, bf16[256,256]{1,0:T(8,128)(2,1)} %convolution_convert_fusion.2.refs_1_, s32[2,128]{1,0:T(2,128)} %bitcast.196), custom_call_target="tpu_custom_call" | custom-call | tf_op jit(solution)/shard_map/shift_on/pallas_call | solution.py:544
  71.0 1.7 slice_bitcast_fusion.3
  79.9 1.0 convolution_convert_fusion.1
  82.5 2.9 %fusion.87 = f32[256,2048]{1,0:T(8,128)S(1)} fusion(bf16[256,640]{1,0:T(8,128)(2,1)S(1)} %multiply_convert_fusion.2.refs_0_.refs_1_, bf16[640,2048]{1,0:T(8,128)(2,1)} %get-tuple-element.45), kind=kOutput, calls=%fused_computation.192 | convolution fusion | flops 671088640 | bytes 5046272 | tf_op jit(solution)/shard_map/dot_general | solution.py:633
  85.4 2.6 multiply_convert_fusion.1
  89.0 1.8 multiply_reduce_fusion.6
  90.9 1.5 fusion.33
  92.4 2.1 fusion.34
  94.5 4.6 %multiply_convert_fusion = (bf16[256,2048]{1,0:T(8,128)(2,1)S(1)}, bf16[256,2048]{1,0:T(8,128)(2,1)S(1)}) fusion(f32[256,2048]{1,0:T(8,128)S(1)} %copy-done.20, f32[256,2048]{1,0:T(8,128)} %get-tuple-element.113, bf16[256,640]{1,0:T(8,128)(2,1)S(1)} %get-tuple-element.80.refs_8_, bf16[2048,640]{1,0:T(8,128)(2,1)} %get-tuple-element.47), kind=kOutput, calls=%fused_computation.19 | convolution fusion | flops 683671552 | bytes 9240576 | tf_op jit(solution)/shard_map/dot_general | solution.py:642
  99.1 1.0 fusion.88
  100.2 1.4 copy-done.16
  101.6 1.4 multiply_reduce_fusion.2
  105.0 2.3 fusion.40
  107.3 7.8 %fusion.16 = f32[768,256]{1,0:T(8,128)} fusion(f32[768,256,4]{1,0,2:T(8,128)} %fusion.40, bf16[256,4,128]{2,0,1:T(8,128)(2,1)} %copy-done.44, bf16[256,4,128]{2,0,1:T(8,128)(2,1)} %copy-done.43, f32[768,256,4]{1,0,2:T(8,128)} %copy-done.11, f32[4,256]{1,0:T(4,128)S(1)} %copy-done.50, pred[256,768]{0,1:T(8,128)(4,1)S(1)} %copy-done.36), kind=kOutput, calls=%fused_computation.32 | convolution fusion | flops 413927168 | bytes 7802880 | tf_op jit(solution)/shard_map/hqk,qhd->kd/dot_general | solution.py:675
  115.1 1.8 slice.134
  116.9 2.8 %convolution_bitcast_fusion = f32[768,256]{1,0:T(8,128)S(1)} fusion(bf16[32,4,8,256]{3,2,1,0:T(8,128)(2,1)S(1)} %bitcast.190, f32[768,256,4]{1,0,2:T(8,128)} %copy-done.11, f32[4,256]{1,0:T(4,128)S(1)} %copy-done.50, pred[256,768]{0,1:T(8,128)(4,1)S(1)} %copy-done.36), kind=kOutput, calls=%fused_computation.34 | convolution fusion | flops 406585344 | bytes 4657152 | tf_op jit(solution)/shard_map/hqk,qhd->kd/dot_general | solution.py:678
  121.4 11.9 %shift_back.1 = (bf16[2,256,256]{2,1,0:T(8,128)(2,1)}, bf16[2,256,256]{2,1,0:T(8,128)(2,1)}) custom-call(bf16[2,256,256]{2,1,0:T(8,128)(2,1)} %bitcast.191, bf16[2,256,256]{2,1,0:T(8,128)(2,1)} %bitcast.192), custom_call_target="tpu_custom_call" | custom-call | tf_op jit(solution)/shard_map/shift_back/pallas_call | solution.py:544
  133.3 1.0 convert_reduce_fusion
  135.3 1.3 fusion.90
  136.7 1.0 convert_reduce_fusion.1
  137.7 1.0 fusion.48
  140.3 1.1 fusion.89
  141.4 8.3 %fusion.15 = f32[256,4,256]{2,0,1:T(8,128)} fusion(f32[768,256,4]{1,0,2:T(8,128)} %fusion.40, bf16[256,256]{1,0:T(8,128)(2,1)} %maximum_bitcast_fusion.6.refs_0_, bf16[256,256]{1,0:T(8,128)(2,1)} %copy-done.47, bf16[256,256]{1,0:T(8,128)(2,1)} %copy-done.46, f32[768,256,4]{1,0,2:T(8,128)} %copy-done.11, f32[4,256]{1,0:T(4,128)S(1)} %copy-done.50, ...), kind=kOutput, calls=%fused_computation.26 | convolution fusion | flops 414058240 | bytes 7933952 | tf_op jit(solution)/shard_map/hqk,kd->qhd/dot_general | solution.py:672
  149.7 1.3 multiply_add_fusion.1
  153.4 1.1 fusion.36
  154.4 1.0 copy.119.refs_5_
  157.9 98.1 %reduce_terms.1 = (bf16[17,2,2,4,80,128]{5,4,3,2,1,0:T(8,128)(2,1)}, f32[4,24,128]{2,1,0:T(8,128)}) custom-call(bf16[256,640]{1,0:T(8,128)(2,1)} %copy-done.2, bf16[256,640]{1,0:T(8,128)(2,1)} %copy-done.2, bf16[256,2048]{1,0:T(8,128)(2,1)} %copy-done.33, bf16[256,640]{1,0:T(8,128)(2,1)} %copy-done, bf16[256,640]{1,0:T(8,128)(2,1)} %copy-done, ...), custom_call_target="tpu_custom_call" | custom-call | tf_op jit(solution)/shard_map/reduce_terms/pallas_call | solution.py:402
  256.1 13.5 %unpack.1 = (f32[320,2048]{1,0:T(8,128)}, f32[320,2048]{1,0:T(8,128)}, f32[1024,640]{1,0:T(8,128)}, f32[320,1024]{1,0:T(8,128)}, f32[320,256]{1,0:T(8,128)}, /*index=5*/f32[320,256]{1,0:T(8,128)}, f32[512,640]{1,0:T(8,128)}) custom-call(bf16[17,2,2,4,80,128]{5,4,3,2,1,0:T(8,128)(2,1)} %get-tuple-element.50.summed), custom_call_target="tpu_custom_call" | custom-call | tf_op jit(solution)/shard_map/unpack/pallas_call | solution.py:479
  (174 shorter events, 25.8 us)
Async XLA Ops:
  0.6 55.7 %copy-start.1 = (bf16[256,640]{1,0:T(8,128)(2,1)S(1)}, bf16[256,640]{1,0:T(8,128)(2,1)}, u32[]{:S(2)}) copy-start(bf16[256,640]{1,0:T(8,128)(2,1)} %param.16) | copy-start | bytes 983044
  55.2 18.2 %copy-start.48 = (s32[256]{0:T(256)S(1)}, s32[256]{0:T(256)}, u32[]{:S(2)}) copy-start(s32[256]{0:T(256)} %param.17) | copy-start | bytes 3076
  55.2 19.2 %copy-start.3 = (bf16[640,1024]{1,0:T(8,128)(2,1)S(1)}, bf16[640,1024]{1,0:T(8,128)(2,1)}, u32[]{:S(2)}) copy-start(bf16[640,1024]{1,0:T(8,128)(2,1)} %get-tuple-element.43) | copy-start | bytes 3932164
  56.6 18.4 %copy-start = (bf16[256,640]{1,0:T(8,128)(2,1)}, bf16[256,640]{1,0:T(8,128)(2,1)S(1)}, u32[]{:S(2)}) copy-start(bf16[256,640]{1,0:T(8,128)(2,1)S(1)} %fusion.30.refs_3_.refs_4_) | copy-start | bytes 983044
  60.1 14.3 %copy-start.8 = (f32[256,256]{1,0:T(8,128)}, f32[256,256]{1,0:T(8,128)S(1)}, u32[]{:S(2)}) copy-start(f32[256,256]{1,0:T(8,128)S(1)} %copy.97) | copy-start | bytes 786436
  74.4 4.9 %copy-start.35 = (pred[256,768]{0,1:T(8,128)(4,1)}, pred[256,768]{0,1:T(8,128)(4,1)S(1)}, u32[]{:S(2)}) copy-start(pred[256,768]{0,1:T(8,128)(4,1)S(1)} %fusion.25) | copy-start | bytes 589828
  75.5 2.2 copy-start.37
  77.0 2.3 copy-start.46
  78.4 2.5 copy-start.11
  82.3 3.1 %copy-start.15 = (bf16[640,2048]{1,0:T(8,128)(2,1)S(1)}, bf16[640,2048]{1,0:T(8,128)(2,1)}, u32[]{:S(2)}) copy-start(bf16[640,2048]{1,0:T(8,128)(2,1)} %get-tuple-element.46) | copy-start | bytes 7864324
  82.5 5.5 %copy-start.2 = (bf16[256,640]{1,0:T(8,128)(2,1)}, bf16[256,640]{1,0:T(8,128)(2,1)S(1)}, u32[]{:S(2)}) copy-start(bf16[256,640]{1,0:T(8,128)(2,1)S(1)} %multiply_convert_fusion.2.refs_0_.refs_1_) | copy-start | bytes 983044
  85.4 2.6 copy-start.19
  85.4 3.6 %copy-start.51 = (bf16[2048,640]{1,0:T(8,128)(2,1)S(1)}, bf16[2048,640]{1,0:T(8,128)(2,1)}, u32[]{:S(2)}) copy-start(bf16[2048,640]{1,0:T(8,128)(2,1)} %get-tuple-element.47) | copy-start | bytes 7864324
  88.0 2.9 %copy-start.13 = (bf16[256,640]{1,0:T(8,128)(2,1)S(1)}, bf16[256,640]{1,0:T(8,128)(2,1)}, u32[]{:S(2)}) copy-start(bf16[256,640]{1,0:T(8,128)(2,1)} %param.31) | copy-start | bytes 983044
  90.9 3.6 %copy-start.20 = (f32[256,2048]{1,0:T(8,128)S(1)}, f32[256,2048]{1,0:T(8,128)}, u32[]{:S(2)}) copy-start(f32[256,2048]{1,0:T(8,128)} %copy-done.19) | copy-start | bytes 6291460
  94.5 4.6 %copy-start.23 = (bf16[256,640]{1,0:T(8,128)(2,1)}, bf16[256,640]{1,0:T(8,128)(2,1)S(1)}, u32[]{:S(2)}) copy-start(bf16[256,640]{1,0:T(8,128)(2,1)S(1)} %get-tuple-element.80.refs_8_) | copy-start | bytes 983044
  94.5 4.6 %copy-start.17 = (bf16[640,2048]{1,0:T(8,128)(2,1)S(1)}, bf16[640,2048]{1,0:T(8,128)(2,1)}, u32[]{:S(2)}) copy-start(bf16[640,2048]{1,0:T(8,128)(2,1)} %get-tuple-element.45) | copy-start | bytes 7864324
  99.1 4.0 %copy-start.10 = (bf16[256,2048]{1,0:T(8,128)(2,1)}, bf16[256,2048]{1,0:T(8,128)(2,1)S(1)}, u32[]{:S(2)}) copy-start(bf16[256,2048]{1,0:T(8,128)(2,1)S(1)} %get-tuple-element.74.refs_7_) | copy-start | bytes 3145732
  99.1 4.0 %copy-start.34 = (bf16[256,2048]{1,0:T(8,128)(2,1)}, bf16[256,2048]{1,0:T(8,128)(2,1)S(1)}, u32[]{:S(2)}) copy-start(bf16[256,2048]{1,0:T(8,128)(2,1)S(1)} %get-tuple-element.75.refs_6_) | copy-start | bytes 3145732
  99.1 2.5 copy-start.16
  100.1 2.9 %copy-start.14 = (bf16[256,640]{1,0:T(8,128)(2,1)S(1)}, bf16[256,640]{1,0:T(8,128)(2,1)}, u32[]{:S(2)}) copy-start(bf16[256,640]{1,0:T(8,128)(2,1)} %param.31) | copy-start | bytes 983044
  103.1 1.9 copy-start.32
  104.4 10.8 %copy-start.12 = (bf16[256,640]{1,0:T(8,128)(2,1)}, bf16[256,640]{1,0:T(8,128)(2,1)S(1)}, u32[]{:S(2)}) copy-start(bf16[256,640]{1,0:T(8,128)(2,1)S(1)} %fusion.35.refs_11_) | copy-start | bytes 983044
  104.4 2.9 %copy-start.36 = (pred[256,768]{0,1:T(8,128)(4,1)S(1)}, pred[256,768]{0,1:T(8,128)(4,1)}, u32[]{:S(2)}) copy-start(pred[256,768]{0,1:T(8,128)(4,1)} %copy-done.35) | copy-start | bytes 589828
  104.4 2.9 %copy-start.50 = (f32[4,256]{1,0:T(4,128)S(1)}, f32[4,256]{1,0:T(4,128)}, u32[]{:S(2)}) copy-start(f32[4,256]{1,0:T(4,128)} %copy-done.49) | copy-start | bytes 12292
  120.6 18.6 %copy-start.9 = (f32[256,256]{1,0:T(8,128)S(1)}, f32[256,256]{1,0:T(8,128)}, u32[]{:S(2)}) copy-start(f32[256,256]{1,0:T(8,128)} %copy-done.8) | copy-start | bytes 786436
  120.6 19.6 %copy-start.24 = (bf16[640,256]{1,0:T(8,128)(2,1)S(1)}, bf16[640,256]{1,0:T(8,128)(2,1)}, u32[]{:S(2)}) copy-start(bf16[640,256]{1,0:T(8,128)(2,1)} %get-tuple-element.38) | copy-start | bytes 983044
  135.3 2.3 copy-start.27
  141.4 8.3 %copy-start.26 = (f32[256,128]{1,0:T(8,128)S(1)}, f32[256,128]{1,0:T(8,128)}, u32[]{:S(2)}) copy-start(f32[256,128]{1,0:T(8,128)} %copy-done.25) | copy-start | bytes 393220
  152.0 2.4 copy-start.7
  152.5 2.9 %copy-start.28 = (bf16[256,256]{1,0:T(8,128)(2,1)S(1)}, bf16[256,256]{1,0:T(8,128)(2,1)}, u32[]{:S(2)}) copy-start(bf16[256,256]{1,0:T(8,128)(2,1)} %copy-done.27) | copy-start | bytes 393220
  152.5 2.9 %copy-start.30 = (bf16[256,256]{1,0:T(8,128)(2,1)S(1)}, bf16[256,256]{1,0:T(8,128)(2,1)}, u32[]{:S(2)}) copy-start(bf16[256,256]{1,0:T(8,128)(2,1)} %copy-done.29) | copy-start | bytes 393220
  (20 other events, 25.8 us)
